TPU v7x, 32 devices: a whole 2x2x4 slice. The times are simulated.
32 devices in a mesh: ctx: 8 (over z, y), shard: 4 (over x, core).
Axes of the slice: x: 2, y: 2, z: 4, core: 2. Of those that a mesh axis runs over, the one named last changes fastest.
Arguments:
- hidden: bfloat16 [4, 2048, 768], P('shard', 'ctx'), may hold values from -6 to 6
- cotangent: bfloat16 [4, 2048, 768], P('shard', 'ctx'), may hold values from -6 to 6
- query_proj: bfloat16 [768, 768], P('shard'), may hold values from -0.0546875 to 0.0546875
- key_proj: bfloat16 [768, 768], P('shard'), may hold values from -0.21875 to 0.21875
- value_proj: bfloat16 [768, 768], P('shard'), may hold values from -0.21875 to 0.21875
- out_proj: bfloat16 [768, 768], P('shard'), may hold values from -0.875 to 0.875
- gate_proj: bfloat16 [768, 2048], P('shard'), may hold values from -0.21875 to 0.21875
- up_proj: bfloat16 [768, 2048], P('shard'), may hold values from -0.21875 to 0.21875
- down_proj: bfloat16 [2048, 768], P('shard'), may hold values from -0.125 to 0.125
- first_gain: bfloat16 [768], P('shard'), may hold values from 0.5 to 1.5
- second_gain: bfloat16 [768], P('shard'), may hold values from 0.5 to 1.5
- global_gain: bfloat16 [768], P('shard'), may hold values from 0.5 to 1.5
- local_bias: bfloat16 [32, 12], P('shard'), may hold values from -4 to 4
- side_bias: bfloat16 [32, 12], P('shard'), may hold values from -4 to 4
- segments: int32 [4, 2048], P('shard'), may hold values from 0 to 1, as said below
- local_buckets: int32 [1023], replicated, may hold values from 0 to 31
- global_buckets: int32 [255], replicated, may hold values from 0 to 31
Outputs:
- outputs: bfloat16 [4, 2048, 768], P('shard', 'ctx')
- grad_hidden: bfloat16 [4, 2048, 768], P('shard', 'ctx')
- grad_query: float32 [768, 768], P('shard')
- grad_key: float32 [768, 768], P('shard')
- grad_value: float32 [768, 768], P('shard')
- grad_out: float32 [768, 768], P('shard')
- grad_gate: float32 [768, 2048], P('shard')
- grad_up: float32 [768, 2048], P('shard')
- grad_down: float32 [2048, 768], P('shard')
- grad_first: float32 [768], P('shard')
- grad_second: float32 [768], P('shard')
- grad_global: float32 [768], P('shard')
- grad_local: float32 [32, 12], P('shard')
- grad_side: float32 [32, 12], P('shard')
Inputs may be any that keep to these rules, and one draw needn't show every extreme that they name: `segments`: segment numbers start at 0 in every sequence, never fall, rise by at most one from token to token, and change only at multiples of 16 tokens: every document is a whole number of 16-token blocks. Every sequence holds exactly max(2, 2) documents.
All inputs are finite; a program needn't handle non-finite values.
Results may differ from a plain program's by a relative error of at most 0.018.
Values may be sent and summed in bfloat16 or wider, within the bound.
No kernel may reach another device: no remote copies, remote signals or barrier semaphores. Data moves between devices by JAX's collectives and lax.ppermute only.
A program may use at most 384 MiB of HBM per device.

v0:
```python
import jax
import jax.numpy as jnp
from jax import lax
from jax.sharding import PartitionSpec as P

H = 12
HD = 64
NB = 32
GB = 16
HALF = 512


EPS = 1e-06
NEG = -1e30
HIGHEST = lax.Precision.HIGHEST


def shifted(value, axis, by):
    length = lax.axis_size(axis)
    pairs = [(i, i + by) for i in range(length) if 0 <= i + by < length]
    return lax.ppermute(value, axis, pairs)


def cut_along(value, dim, length):
    before, after = (value.shape[:dim], value.shape[dim + 1 :])
    return jnp.moveaxis(value.reshape(*before, length, -1, *after), dim, 0)


def sum_at_owner(value, axis, dim):
    length = lax.axis_size(axis)
    blocks = lax.all_to_all(cut_along(value, dim, length), axis, 0, 0, tiled=True)
    return jnp.sum(blocks.astype(jnp.float32), axis=0)


def side_by_side(arrays, axis, dim, along):
    both = jnp.concatenate(arrays, axis=along)
    filled, at, done = (sum_at_owner(both, axis, dim), 0, [])
    for a in arrays:
        done.append(lax.slice_in_dim(filled, at, at + a.shape[along], axis=along))
        at += a.shape[along]
    return tuple(done)


def apply_weight(left, right):
    return lax.dot_general(
        left, right, (((left.ndim - 1,), (0,)), ((), ())), preferred_element_type=jnp.float32
    )


def apply_transpose(left, right):
    return lax.dot_general(
        left, right, (((left.ndim - 1,), (1,)), ((), ())), preferred_element_type=jnp.float32
    )


def exact_transpose(left, right):
    return lax.dot_general(
        left, right.astype(jnp.float32), (((left.ndim - 1,), (1,)), ((), ())), precision=HIGHEST
    )


def token_outer(left, right):
    left_rows = left.reshape(-1, left.shape[-1])
    right_rows = right.reshape(-1, right.shape[-1])
    return lax.dot_general(
        left_rows, right_rows, (((0,), (0,)), ((), ())), preferred_element_type=jnp.float32
    )


def exact_outer(left, right):
    left_rows = left.reshape(-1, left.shape[-1]).astype(jnp.float32)
    right_rows = right.reshape(-1, right.shape[-1])
    return lax.dot_general(left_rows, right_rows, (((0,), (0,)), ((), ())), precision=HIGHEST)


def rms_scale(values):
    return lax.rsqrt(jnp.mean(values * values, axis=-1, keepdims=True) + EPS)


def norm_back(upstream, normed_val, row_scale, gain_row):
    scaled = upstream * gain_row
    return row_scale * (scaled - normed_val * jnp.mean(scaled * normed_val, axis=-1, keepdims=True))


def gelu_tanh(values):
    return jax.nn.gelu(values, approximate=True)


def round_trip(values):
    return lax.optimization_barrier(values.astype(jnp.bfloat16)).astype(jnp.float32)


def diagonal_sums(matrix):
    head_count, row_count, col_count = matrix.shape
    flipped = jnp.pad(matrix[:, ::-1, :], ((0, 0), (0, 0), (0, row_count)))
    length = row_count * (col_count + row_count) - row_count
    skewed = flipped.reshape(head_count, -1)[:, :length]
    return jnp.sum(skewed.reshape(head_count, row_count, col_count + row_count - 1), axis=1)


def on_device(
    hidden,
    cotangent,
    query_proj,
    key_proj,
    value_proj,
    out_proj,
    gate_proj,
    up_proj,
    down_proj,
    first_gain,
    second_gain,
    global_gain,
    local_bias,
    side_bias,
    segments,
    local_buckets,
    global_buckets,
):
    seq_count, block_len, model_width = hidden.shape
    cycle_size = lax.axis_size("ctx")
    cycle_index = lax.axis_index("ctx")
    first_row = cycle_index * block_len
    global_count = block_len * cycle_size // GB
    own_blocks = block_len // GB
    reach_steps = HALF // block_len
    window_len = block_len + 2 * HALF
    params = (
        query_proj,
        key_proj,
        value_proj,
        out_proj,
        gate_proj,
        up_proj,
        down_proj,
        first_gain,
        second_gain,
        global_gain,
        local_bias,
        side_bias,
    )
    gathered = (
        lax.all_gather(params[0], "shard", axis=0, tiled=True),
        lax.all_gather(params[1], "shard", axis=0, tiled=True),
        lax.all_gather(params[2], "shard", axis=0, tiled=True),
        lax.all_gather(params[3], "shard", axis=0, tiled=True),
        lax.all_gather(params[4], "shard", axis=0, tiled=True),
        lax.all_gather(params[5], "shard", axis=0, tiled=True),
        lax.all_gather(params[6], "shard", axis=0, tiled=True),
        lax.all_gather(params[7], "shard", axis=0, tiled=True),
        lax.all_gather(params[8], "shard", axis=0, tiled=True),
        lax.all_gather(params[9], "shard", axis=0, tiled=True),
        lax.all_gather(params[10], "shard", axis=0, tiled=True),
        lax.all_gather(params[11], "shard", axis=0, tiled=True),
    )
    (
        w_query,
        w_key,
        w_value,
        w_out,
        w_gate,
        w_up,
        w_down,
        gain_one,
        gain_two,
        gain_side,
        table_near,
        table_side,
    ) = gathered
    inputs = hidden.astype(jnp.float32)
    scale_one = rms_scale(inputs)
    normed_one = inputs * scale_one
    normed = (normed_one * gain_one.astype(jnp.float32)).astype(jnp.bfloat16)
    queries = apply_weight(normed, w_query).astype(jnp.bfloat16)
    keys = apply_weight(normed, w_key).astype(jnp.bfloat16)
    values = apply_weight(normed, w_value).astype(jnp.bfloat16)
    block_sums = jnp.sum(
        normed.astype(jnp.float32).reshape(seq_count, own_blocks, GB, model_width), axis=2
    )
    scale_side = rms_scale(block_sums)
    normed_side = block_sums * scale_side
    side_rows = (normed_side * gain_side.astype(jnp.float32)).astype(jnp.bfloat16)
    all_rows = lax.all_gather(side_rows, "ctx", axis=1, tiled=True)
    side_keys = apply_weight(all_rows, w_key).astype(jnp.bfloat16)
    side_values = apply_weight(all_rows, w_value).astype(jnp.bfloat16)
    left_keys, left_values, right_keys, right_values = ([], [], [], [])
    for distance in range(1, reach_steps + 1):
        for direction in (1, -1):
            moved_keys, moved_values = shifted((keys, values), "ctx", direction * distance)
            if direction == 1:
                left_keys.append(moved_keys)
                left_values.append(moved_values)
            else:
                right_keys.append(moved_keys)
                right_values.append(moved_values)
    window_keys = jnp.concatenate(left_keys[::-1] + [keys] + right_keys, axis=1)
    window_values = jnp.concatenate(left_values[::-1] + [values] + right_values, axis=1)
    bucket_iota = jnp.arange(NB, dtype=jnp.int32)[None, :]
    onehot_near = (local_buckets[:, None] == bucket_iota).astype(jnp.float32)
    onehot_side = (global_buckets[:, None] == bucket_iota).astype(jnp.float32)
    near_table = jnp.dot(onehot_near, table_near.astype(jnp.float32), precision=HIGHEST)
    side_table = jnp.dot(onehot_side, table_side.astype(jnp.float32), precision=HIGHEST)
    row_iota = jnp.arange(block_len, dtype=jnp.int32)[:, None]
    col_iota = jnp.arange(window_len, dtype=jnp.int32)[None, :]
    offsets = col_iota - HALF - row_iota
    near_index = jnp.clip(offsets + HALF - 1, 0, 2 * HALF - 2)
    near_bias = jnp.transpose(jnp.take(near_table, near_index, axis=0), (2, 0, 1))
    global_iota = jnp.arange(global_count, dtype=jnp.int32)[None, :]
    side_index = global_iota - (first_row + row_iota) // GB + global_count - 1
    far_bias = jnp.transpose(jnp.take(side_table, side_index, axis=0), (2, 0, 1))
    label_query = lax.dynamic_slice_in_dim(segments, first_row, block_len, 1)
    label_pad = jnp.pad(segments, ((0, 0), (HALF, HALF)), constant_values=-1)
    label_window = lax.dynamic_slice_in_dim(label_pad, first_row, window_len, 1)
    mask_near = (jnp.abs(offsets) < HALF)[None] & (
        label_window[:, None, :] == label_query[:, :, None]
    )
    mask_far = segments[:, ::GB][:, None, :] == label_query[:, :, None]

    def both_scores(query_block, key_block, side_key, near_mask, far_mask):
        query_heads = query_block.reshape(block_len, H, HD)
        near_scores = (
            jnp.einsum(
                "ihd,jhd->hij",
                query_heads,
                key_block.reshape(window_len, H, HD),
                preferred_element_type=jnp.float32,
            )
            + near_bias
        )
        far_scores = (
            jnp.einsum(
                "ihd,jhd->hij",
                query_heads,
                side_key.reshape(global_count, H, HD),
                preferred_element_type=jnp.float32,
            )
            + far_bias
        )
        near_scores = jnp.where(near_mask[None], near_scores, NEG)
        far_scores = jnp.where(far_mask[None], far_scores, NEG)
        return (query_heads, near_scores, far_scores)

    def forward_sequence(pieces):
        query_block, key_block, value_block, side_key, side_value, near_mask, far_mask = pieces
        query_heads, near_scores, far_scores = both_scores(
            query_block, key_block, side_key, near_mask, far_mask
        )
        peak = jnp.maximum(jnp.max(near_scores, axis=-1), jnp.max(far_scores, axis=-1))
        total = jnp.sum(jnp.exp(near_scores - peak[..., None]), axis=-1) + jnp.sum(
            jnp.exp(far_scores - peak[..., None]), axis=-1
        )
        logsum = peak + jnp.log(total)
        near_probs = jnp.exp(near_scores - logsum[..., None]).astype(jnp.bfloat16)
        far_probs = jnp.exp(far_scores - logsum[..., None]).astype(jnp.bfloat16)
        mixed = jnp.einsum(
            "hij,jhd->ihd",
            near_probs,
            value_block.reshape(window_len, H, HD),
            preferred_element_type=jnp.float32,
        )
        mixed = mixed + jnp.einsum(
            "hij,jhd->ihd",
            far_probs,
            side_value.reshape(global_count, H, HD),
            preferred_element_type=jnp.float32,
        )
        return (mixed.reshape(block_len, model_width).astype(jnp.bfloat16), logsum)

    attended, logsums = lax.map(
        forward_sequence,
        (queries, window_keys, window_values, side_keys, side_values, mask_near, mask_far),
    )
    middle = inputs + apply_weight(attended, w_out)
    scale_two = rms_scale(middle)
    normed_two = middle * scale_two
    ffn_in = (normed_two * gain_two.astype(jnp.float32)).astype(jnp.bfloat16)
    gate_pre = apply_weight(ffn_in, w_gate)
    up_pre = apply_weight(ffn_in, w_up)
    gelu_out, gelu_pull = jax.vjp(gelu_tanh, gate_pre)
    product = (gelu_out * up_pre).astype(jnp.bfloat16)
    outputs = (middle + apply_weight(product, w_down)).astype(jnp.bfloat16)
    regathered = (
        lax.all_gather(params[0], "shard", axis=0, tiled=True),
        lax.all_gather(params[1], "shard", axis=0, tiled=True),
        lax.all_gather(params[2], "shard", axis=0, tiled=True),
        lax.all_gather(params[3], "shard", axis=0, tiled=True),
        lax.all_gather(params[4], "shard", axis=0, tiled=True),
        lax.all_gather(params[5], "shard", axis=0, tiled=True),
        lax.all_gather(params[6], "shard", axis=0, tiled=True),
        lax.all_gather(params[7], "shard", axis=0, tiled=True),
        lax.all_gather(params[8], "shard", axis=0, tiled=True),
        lax.all_gather(params[9], "shard", axis=0, tiled=True),
        lax.all_gather(params[10], "shard", axis=0, tiled=True),
        lax.all_gather(params[11], "shard", axis=0, tiled=True),
    )
    (
        w_query,
        w_key,
        w_value,
        w_out,
        w_gate,
        w_up,
        w_down,
        gain_one,
        gain_two,
        gain_side,
        table_near,
        table_side,
    ) = regathered
    down_grad = token_outer(product, cotangent)
    product_grad = round_trip(apply_transpose(cotangent, w_down))
    gate_delta = gelu_pull(product_grad * up_pre)[0].astype(jnp.bfloat16)
    up_delta = (product_grad * gelu_out).astype(jnp.bfloat16)
    gate_grad = token_outer(ffn_in, gate_delta)
    up_grad = token_outer(ffn_in, up_delta)
    ffn_back = apply_transpose(gate_delta, w_gate) + apply_transpose(up_delta, w_up)
    second_part = jnp.sum(ffn_back * normed_two, axis=(0, 1))
    middle_grad = cotangent.astype(jnp.float32) + norm_back(
        ffn_back, normed_two, scale_two, gain_two.astype(jnp.float32)
    )
    mixed_grad = middle_grad.astype(jnp.bfloat16)
    out_grad = token_outer(attended, mixed_grad)
    attended_grad = apply_transpose(mixed_grad, w_out).astype(jnp.bfloat16)

    def backward_sequence(carry, pieces):
        near_total, far_total = carry
        (
            query_block,
            key_block,
            value_block,
            side_key,
            side_value,
            near_mask,
            far_mask,
            logsum,
            grad_block,
        ) = pieces
        query_heads, near_scores, far_scores = both_scores(
            query_block, key_block, side_key, near_mask, far_mask
        )
        near_probs = jnp.exp(near_scores - logsum[..., None])
        far_probs = jnp.exp(far_scores - logsum[..., None])
        grad_heads = grad_block.reshape(block_len, H, HD)
        key_heads = key_block.reshape(window_len, H, HD)
        side_heads = side_key.reshape(global_count, H, HD)
        near_dprob = jnp.einsum(
            "ihd,jhd->hij",
            grad_heads,
            value_block.reshape(window_len, H, HD),
            preferred_element_type=jnp.float32,
        )
        far_dprob = jnp.einsum(
            "ihd,jhd->hij",
            grad_heads,
            side_value.reshape(global_count, H, HD),
            preferred_element_type=jnp.float32,
        )
        center = jnp.sum(near_probs * near_dprob, axis=-1) + jnp.sum(far_probs * far_dprob, axis=-1)
        near_delta = (near_probs * (near_dprob - center[..., None])).astype(jnp.bfloat16)
        far_delta = (far_probs * (far_dprob - center[..., None])).astype(jnp.bfloat16)
        query_back = jnp.einsum(
            "hij,jhd->ihd", near_delta, key_heads, preferred_element_type=jnp.float32
        )
        query_back = query_back + jnp.einsum(
            "hij,jhd->ihd", far_delta, side_heads, preferred_element_type=jnp.float32
        )
        key_back = jnp.einsum(
            "hij,ihd->jhd", near_delta, query_heads, preferred_element_type=jnp.float32
        )
        value_back = jnp.einsum(
            "hij,ihd->jhd",
            near_probs.astype(jnp.bfloat16),
            grad_heads,
            preferred_element_type=jnp.float32,
        )
        side_key_back = jnp.einsum(
            "hij,ihd->jhd", far_delta, query_heads, preferred_element_type=jnp.float32
        )
        side_value_back = jnp.einsum(
            "hij,ihd->jhd",
            far_probs.astype(jnp.bfloat16),
            grad_heads,
            preferred_element_type=jnp.float32,
        )
        near_total = near_total + near_delta.astype(jnp.float32)
        far_total = far_total + jnp.sum(
            far_delta.astype(jnp.float32).reshape(H, own_blocks, GB, global_count), axis=2
        )
        results = (
            query_back.reshape(block_len, model_width).astype(jnp.bfloat16),
            key_back.reshape(window_len, model_width),
            value_back.reshape(window_len, model_width),
            side_key_back.reshape(global_count, model_width),
            side_value_back.reshape(global_count, model_width),
        )
        return ((near_total, far_total), results)

    carry_start = (
        jnp.zeros((H, block_len, window_len), jnp.float32),
        jnp.zeros((H, own_blocks, global_count), jnp.float32),
    )
    (near_total, far_total), backs = lax.scan(
        backward_sequence,
        carry_start,
        (
            queries,
            window_keys,
            window_values,
            side_keys,
            side_values,
            mask_near,
            mask_far,
            logsums,
            attended_grad,
        ),
    )
    query_delta, key_window_grad, value_window_grad, side_key_part, side_value_part = backs
    own_start = reach_steps * block_len
    key_total = key_window_grad[:, own_start : own_start + block_len]
    value_total = value_window_grad[:, own_start : own_start + block_len]
    for distance in range(1, reach_steps + 1):
        for direction in (1, -1):
            piece_start = (reach_steps - direction * distance) * block_len
            back_keys, back_values = (
                shifted(
                    key_window_grad[:, piece_start : piece_start + block_len].astype(jnp.bfloat16),
                    "ctx",
                    -direction * distance,
                ).astype(jnp.float32),
                shifted(
                    value_window_grad[:, piece_start : piece_start + block_len].astype(
                        jnp.bfloat16
                    ),
                    "ctx",
                    -direction * distance,
                ).astype(jnp.float32),
            )
            key_total = key_total + back_keys
            value_total = value_total + back_values
    key_delta = key_total.astype(jnp.bfloat16)
    value_delta = value_total.astype(jnp.bfloat16)
    query_grad = token_outer(normed, query_delta)
    key_grad = token_outer(normed, key_delta)
    value_grad = token_outer(normed, value_delta)
    side_key_delta, side_value_delta = side_by_side(
        (side_key_part.astype(jnp.bfloat16), side_value_part.astype(jnp.bfloat16)), "ctx", 1, 0
    )
    key_grad = key_grad + exact_outer(side_rows, side_key_delta)
    value_grad = value_grad + exact_outer(side_rows, side_value_delta)
    side_back = exact_transpose(side_key_delta, w_key) + exact_transpose(side_value_delta, w_value)
    global_part = jnp.sum(side_back * normed_side, axis=(0, 1))
    sums_grad = norm_back(side_back, normed_side, scale_side, gain_side.astype(jnp.float32))
    normed_back = (
        apply_transpose(query_delta, w_query)
        + apply_transpose(key_delta, w_key)
        + apply_transpose(value_delta, w_value)
    )
    normed_back = (
        normed_back.reshape(seq_count, own_blocks, GB, model_width) + sums_grad[:, :, None, :]
    ).reshape(seq_count, block_len, model_width)
    first_part = jnp.sum(normed_back * normed_one, axis=(0, 1))
    hidden_grad = (
        middle_grad + norm_back(normed_back, normed_one, scale_one, gain_one.astype(jnp.float32))
    ).astype(jnp.bfloat16)
    near_diag = diagonal_sums(near_total)
    near_grad = near_diag[:, block_len : block_len + 2 * HALF - 1]
    local_part = lax.dot_general(
        onehot_near, near_grad, (((0,), (1,)), ((), ())), precision=HIGHEST
    )
    far_diag = diagonal_sums(far_total)
    place_start = global_count - own_blocks - first_row // GB
    side_rel = lax.dynamic_update_slice(
        jnp.zeros((H, 2 * global_count - 1), jnp.float32), far_diag, (jnp.int32(0), place_start)
    )
    side_part = lax.dot_general(onehot_side, side_rel, (((0,), (1,)), ((), ())), precision=HIGHEST)
    partials = (
        query_grad,
        key_grad,
        value_grad,
        out_grad,
        gate_grad,
        up_grad,
        down_grad,
        first_part,
        second_part,
        global_part,
        local_part,
        side_part,
    )
    shared = (
        lax.psum_scatter(
            partials[0].astype(jnp.bfloat16), "shard", scatter_dimension=0, tiled=True
        ).astype(jnp.float32),
        lax.psum_scatter(
            partials[1].astype(jnp.bfloat16), "shard", scatter_dimension=0, tiled=True
        ).astype(jnp.float32),
        lax.psum_scatter(
            partials[2].astype(jnp.bfloat16), "shard", scatter_dimension=0, tiled=True
        ).astype(jnp.float32),
        lax.psum_scatter(
            partials[3].astype(jnp.bfloat16), "shard", scatter_dimension=0, tiled=True
        ).astype(jnp.float32),
        lax.psum_scatter(
            partials[4].astype(jnp.bfloat16), "shard", scatter_dimension=0, tiled=True
        ).astype(jnp.float32),
        lax.psum_scatter(
            partials[5].astype(jnp.bfloat16), "shard", scatter_dimension=0, tiled=True
        ).astype(jnp.float32),
        lax.psum_scatter(
            partials[6].astype(jnp.bfloat16), "shard", scatter_dimension=0, tiled=True
        ).astype(jnp.float32),
        lax.psum_scatter(
            partials[7].astype(jnp.bfloat16), "shard", scatter_dimension=0, tiled=True
        ).astype(jnp.float32),
        lax.psum_scatter(
            partials[8].astype(jnp.bfloat16), "shard", scatter_dimension=0, tiled=True
        ).astype(jnp.float32),
        lax.psum_scatter(
            partials[9].astype(jnp.bfloat16), "shard", scatter_dimension=0, tiled=True
        ).astype(jnp.float32),
        lax.psum_scatter(
            partials[10].astype(jnp.bfloat16), "shard", scatter_dimension=0, tiled=True
        ).astype(jnp.float32),
        lax.psum_scatter(
            partials[11].astype(jnp.bfloat16), "shard", scatter_dimension=0, tiled=True
        ).astype(jnp.float32),
    )
    totals = lax.psum(
        (
            shared[0],
            shared[1],
            shared[2],
            shared[3],
            shared[4],
            shared[5],
            shared[6],
            shared[7],
            shared[8],
            shared[9],
            shared[10],
            shared[11],
        ),
        "ctx",
    )
    return (
        outputs,
        hidden_grad,
        totals[0],
        totals[1],
        totals[2],
        totals[3],
        totals[4],
        totals[5],
        totals[6],
        totals[7],
        totals[8],
        totals[9],
        totals[10],
        totals[11],
    )


def solution(mesh):
    return jax.shard_map(
        on_device,
        mesh=mesh,
        in_specs=(
            P("shard", "ctx", None),
            P("shard", "ctx", None),
            P("shard", None),
            P("shard", None),
            P("shard", None),
            P("shard", None),
            P("shard", None),
            P("shard", None),
            P("shard", None),
            P("shard"),
            P("shard"),
            P("shard"),
            P("shard", None),
            P("shard", None),
            P("shard", None),
            P(),
            P(),
        ),
        out_specs=(
            P("shard", "ctx", None),
            P("shard", "ctx", None),
            P("shard", None),
            P("shard", None),
            P("shard", None),
            P("shard", None),
            P("shard", None),
            P("shard", None),
            P("shard", None),
            P("shard"),
            P("shard"),
            P("shard"),
            P("shard", None),
            P("shard", None),
        ),
        check_vma=False,
    )
```

profile of v0, /device:TPU:0, one launch (start us, length us, event | category | flops | bytes accessed | tf_op | source)
XLA Modules:
  0.0 2158.3 jit_solution(9509631542682910207)
XLA Ops:
  14.0 9.1 all-reduce.13
  28.1 5.2 all_gather.53
  33.6 1074.8 %gather_fusion = f32[327680,12]{1,0:T(8,128)} fusion(f32[1023,12]{1,0:T(8,128)S(1)} %fusion.66, s32[327680]{0:T(1024)S(1)} %broadcast_clamp_fusion), kind=kCustom, calls=%fused_computation | custom fusion | bytes 32768000 | tf_op jit(solution)/shard_map/jit(_take)/gather | solution.py:207
  1108.4 89.6 %copy.121 = f32[256,1280,12]{1,0,2:T(8,128)} copy(f32[256,1280,12]{2,1,0:T(8,128)} %bitcast.16) | data formatting | bytes 31457280 | tf_op jit(solution)/shard_map/jit(_take)/gather | solution.py:207
  1199.2 31.0 %all_gather.55 = bf16[1,128,768]{2,1,0:T(8,128)(2,1)S(1)} all-gather(bf16[1,16,768]{2,1,0:T(8,128)(2,1)S(1)} %fusion.102), channel_id=1, replica_groups=mesh['ctx'=8,'shard'=4] {'ctx'}, dimensions={1}, use_global_device_ids=true | all-gather | bytes 221184 | tf_op jit(solution)/shard_map/all_gather | solution.py:183
  1232.9 5.2 all_gather.56
  1238.3 108.2 %gather_fusion.1 = f32[32768,12]{1,0:T(8,128)} fusion(f32[255,12]{1,0:T(8,128)S(1)} %fusion.93, s32[32768]{0:T(1024)S(1)} %fusion.91), kind=kCustom, calls=%fused_computation.1 | custom fusion | bytes 3276800 | tf_op jit(solution)/shard_map/jit(_take)/gather | solution.py:210
  1346.5 10.7 copy.122
  1357.8 2.6 convolution_convert_fusion.7
  1362.4 4.1 collective-permute-start.5
  1373.0 2.5 convolution_convert_fusion.9
  1379.0 5.3 collective-permute-start
  1386.7 5.3 collective-permute-start.1
  1411.5 11.5 fusion.112
  1433.9 7.8 exponential_reduce_fusion
  1443.2 8.1 fusion.31
  1454.5 4.0 fusion.2
  1458.6 4.2 fusion.114
  1462.7 4.9 multiply_convert_fusion.1
  1478.2 11.8 multiply_reduce_fusion
  1490.1 2.7 multiply_reduce_fusion.1
  1495.0 14.5 multiply_convert_fusion
  1509.5 2.5 convert_reduce_fusion
  1523.2 8.3 all-to-all-start
  1532.9 6.3 fusion.30
  1541.5 9.9 fusion.14
  1551.5 2.3 bitcast_convert_fusion
  1555.3 4.6 collective-permute-start.13
  1561.1 5.0 collective-permute-start.15
  1566.1 7.3 collective-permute-done.13
  1579.8 4.7 fusion.117
  1586.2 4.6 collective-permute-start.11
  1592.0 5.7 collective-permute-start.9
  1597.9 5.0 collective-permute-done.8
  1602.9 9.1 collective-permute-done.9
  1615.1 4.6 convolution_convert_fusion.1
  1621.1 2.7 convolution_convert_fusion.2
  1625.1 2.7 convolution_convert_fusion
  1628.9 113.8 %rev.6 = f32[12,256,1280]{2,1,0:T(8,128)} reverse(bf16[12,256,1280]{2,1,0:T(8,128)(2,1)} %multiply_convert_fusion), dimensions={1} | reverse | bytes 23592960 | tf_op jit(solution)/shard_map/rev | solution.py:95
  1742.8 12.0 pad.13
  1754.8 9.2 pad.19
  1764.0 16.9 copy.123
  1780.9 17.0 slice.91
  1797.9 31.1 %reshape.757 = f32[12,256,1535]{2,1,0:T(8,128)} reshape(f32[12,392960]{1,0:T(8,128)} %slice.91) | data formatting | bytes 37724160 | tf_op jit(solution)/shard_map/reshape | solution.py:98
  1829.0 9.0 reduce_sum.185
  1852.1 3.7 fusion.29
  1860.0 10.3 all-reduce.12
  1871.6 279.9 %all-reduce.15 = (f32[192,768]{1,0:T(8,128)}, f32[192,768]{1,0:T(8,128)}, f32[192,768]{1,0:T(8,128)}, f32[192,768]{1,0:T(8,128)}, f32[192,2048]{1,0:T(8,128)}, /...) all-reduce(bf16[192,768]{1,0:T(8,128)(2,1)} %reduce-scatter.8.clone, ...), channel_id=1, replica_groups=mesh['ctx'=8,'shard'=4] {'ctx'}, use_global_device_ids=true, to_apply=%region_15.16 | all-reduce | flops 1770240 | bytes 10622976 | tf_op jit(solution)/shard_map/psum | solution.py:528
  (330 shorter events, 129.8 us)
Async XLA Ops:
  7.2 1350.6 %all-gather.12.cloned.1.call-start = ((), (), s32[]{:S(2)}) async-start(), calls=%async_computation.10 | async-start | bytes 1474560 | tf_op jit(solution)/shard_map/all_gather | solution.py:144
  8.0 1363.4 %all-gather.8.cloned.1.call-start = ((), (), s32[]{:S(2)}) async-start(), calls=%async_computation.8 | async-start | bytes 1474560 | tf_op jit(solution)/shard_map/all_gather | solution.py:145
  8.7 1366.8 %all-gather.10.cloned.1.call-start = ((), (), s32[]{:S(2)}) async-start(), calls=%async_computation.9 | async-start | bytes 1474560 | tf_op jit(solution)/shard_map/all_gather | solution.py:143
  9.5 1442.0 %all-gather.14.cloned.1.call-start = ((), (), s32[]{:S(2)}) async-start(), calls=%async_computation.11 | async-start | bytes 1474560 | tf_op jit(solution)/shard_map/all_gather | solution.py:146
  10.0 1444.5 %all-gather.20.cloned.1.call-start = ((), (), s32[]{:S(2)}) async-start(), calls=%async_computation.14 | async-start | bytes 3932160 | tf_op jit(solution)/shard_map/all_gather | solution.py:149
  10.6 1447.9 %all-gather.16.cloned.1.call-start = ((), (), s32[]{:S(2)}) async-start(), calls=%async_computation.12 | async-start | bytes 3932160 | tf_op jit(solution)/shard_map/all_gather | solution.py:147
  11.2 1451.5 %all-gather.18.cloned.1.call-start = ((), (), s32[]{:S(2)}) async-start(), calls=%async_computation.13 | async-start | bytes 3932160 | tf_op jit(solution)/shard_map/all_gather | solution.py:148
  12.0 1859.6 %reduce-scatter.14.cloned.1.call-start = ((), (), s32[]{:S(2)}) async-start(), calls=%async_computation.18 | async-start | bytes 1474560 | tf_op jit(solution)/shard_map/reduce_scatter | solution.py:500
  1108.4 89.7 %copy-start.4 = (bf16[1,256,768]{2,1,0:T(8,128)(2,1)S(1)}, bf16[1,256,768]{2,1,0:T(8,128)(2,1)}, u32[]{:S(2)}) copy-start(bf16[1,256,768]{2,1,0:T(8,128)(2,1)} %param.17) | copy-start | bytes 1179652
  1108.4 89.7 %copy-start.46 = (f32[768]{0:T(1024)S(1)}, f32[768]{0:T(1024)}, u32[]{:S(2)}) copy-start(f32[768]{0:T(1024)} %convert_element_type.315) | copy-start | bytes 9220
  1108.4 89.7 %copy-start.51 = (f32[256]{0:T(256)S(1)}, f32[256]{0:T(256)}, u32[]{:S(2)}) copy-start(f32[256]{0:T(256)} %add_rsqrt_fusion.1) | copy-start | bytes 3076
  1108.4 90.2 %copy-start.65 = (bf16[768]{0:T(1024)(128)(2,1)S(1)}, bf16[768]{0:T(1024)(128)(2,1)}, u32[]{:S(2)}) copy-start(bf16[768]{0:T(1024)(128)(2,1)} %get-tuple-element.131) | copy-start | bytes 4612
  1108.4 121.7 %copy-start.61 = (s32[256]{0:T(256)S(1)}, s32[256]{0:T(256)}, u32[]{:S(2)}) copy-start(s32[256]{0:T(256)} %and_select_fusion) | copy-start | bytes 3076
  1108.4 121.8 %copy-start.45 = (s32[1280]{0:T(1024)S(1)}, s32[1280]{0:T(1024)}, u32[]{:S(2)}) copy-start(s32[1280]{0:T(1024)} %copy-done.44) | copy-start | bytes 15364
  1108.4 121.8 %copy-start.50 = (s32[1280]{0:T(1024)S(1)}, s32[1280]{0:T(1024)}, u32[]{:S(2)}) copy-start(s32[1280]{0:T(1024)} %fusion.106) | copy-start | bytes 15364
  1108.4 121.8 %copy-start.56 = (s32[1,256]{1,0:T(1,128)S(1)}, s32[1,256]{1,0:T(1,128)}, u32[]{:S(2)}) copy-start(s32[1,256]{1,0:T(1,128)} %constant_dynamic-slice_fusion) | copy-start | bytes 3076
  1198.1 34.1 %copy-start.69 = (s32[1,128]{1,0:T(1,128)S(1)}, s32[1,128]{1,0:T(1,128)}, u32[]{:S(2)}) copy-start(s32[1,128]{1,0:T(1,128)} %slice.58) | copy-start | bytes 1540
  1198.1 34.8 %copy-start.63 = (bf16[8,12]{1,0:T(8,128)(2,1)S(1)}, bf16[8,12]{1,0:T(8,128)(2,1)}, u32[]{:S(2)}) copy-start(bf16[8,12]{1,0:T(8,128)(2,1)} %param.30) | copy-start | bytes 580
  1198.1 40.0 %copy-start.68 = (s32[255]{0:T(256)S(1)}, s32[255]{0:T(256)}, u32[]{:S(2)}) copy-start(s32[255]{0:T(256)} %param.33) | copy-start | bytes 3064
  1198.4 34.5 %copy-start.28 = (f32[16,768]{1,0:T(8,128)}, f32[16,768]{1,0:T(8,128)S(1)}, u32[]{:S(2)}) copy-start(f32[16,768]{1,0:T(8,128)S(1)} %convert_reduce_fusion.1) | copy-start | bytes 147460
  1198.6 148.0 %copy-start.53 = (f32[16]{0:T(128)}, f32[16]{0:T(128)S(1)}, u32[]{:S(2)}) copy-start(f32[16]{0:T(128)S(1)} %add_rsqrt_fusion.2) | copy-start | bytes 196
  1360.4 26.2 %collective-permute-start.4 = (bf16[1,256,768]{2,1,0:T(8,128)(2,1)}, bf16[1,256,768]{2,1,0:T(8,128)(2,1)}, u32[]{:S(2)}, u32[]{:S(2)}) collective-permute-start(bf16[1,256,768]{2,1,0:T(8,128)(2,1)} %bitcast.10), channel_id=1, source_target_pairs={{0,8},{4,12},{8,16},{12,20},{16,24},{20,28},{1,9},{5,13},{9,17},{1... | collective-permute-start | bytes 1179656 | tf_op jit(solution)/shard_map/ppermute | solution.py:21
  1362.4 33.3 %collective-permute-start.5 = (bf16[1,256,768]{2,1,0:T(8,128)(2,1)}, bf16[1,256,768]{2,1,0:T(8,128)(2,1)}, u32[]{:S(2)}, u32[]{:S(2)}) collective-permute-start(bf16[1,256,768]{2,1,0:T(8,128)(2,1)} %bitcast.10), channel_id=1, source_target_pairs={{0,4},{4,8},{8,12},{12,16},{16,20},{20,24},{24,28},{1,5},{5,9},{9,... | collective-permute-start | bytes 1179656 | tf_op jit(solution)/shard_map/ppermute | solution.py:21
  1368.4 30.5 %collective-permute-start.6 = (bf16[1,256,768]{2,1,0:T(8,128)(2,1)}, bf16[1,256,768]{2,1,0:T(8,128)(2,1)}, u32[]{:S(2)}, u32[]{:S(2)}) collective-permute-start(bf16[1,256,768]{2,1,0:T(8,128)(2,1)} %bitcast.10), channel_id=1, source_target_pairs={{4,0},{8,4},{12,8},{16,12},{20,16},{24,20},{28,24},{5,1},{9,5},{13... | collective-permute-start | bytes 1179656 | tf_op jit(solution)/shard_map/ppermute | solution.py:21
  1369.7 38.1 %collective-permute-start.7 = (bf16[1,256,768]{2,1,0:T(8,128)(2,1)}, bf16[1,256,768]{2,1,0:T(8,128)(2,1)}, u32[]{:S(2)}, u32[]{:S(2)}) collective-permute-start(bf16[1,256,768]{2,1,0:T(8,128)(2,1)} %bitcast.10), channel_id=1, source_target_pairs={{8,0},{12,4},{16,8},{20,12},{24,16},{28,20},{9,1},{13,5},{17,9},{2... | collective-permute-start | bytes 1179656 | tf_op jit(solution)/shard_map/ppermute | solution.py:21
  1377.8 63.9 %copy-start.31 = (bf16[128,768]{0,1:T(8,128)(2,1)}, bf16[128,768]{0,1:T(8,128)(2,1)S(1)}, u32[]{:S(2)}) copy-start(bf16[128,768]{0,1:T(8,128)(2,1)S(1)} %copy.114) | copy-start | bytes 589828
  1379.0 44.0 %collective-permute-start = (bf16[1,256,768]{2,1,0:T(8,128)(2,1)}, bf16[1,256,768]{2,1,0:T(8,128)(2,1)}, u32[]{:S(2)}, u32[]{:S(2)}) collective-permute-start(bf16[1,256,768]{2,1,0:T(8,128)(2,1)} %bitcast.2), channel_id=1, source_target_pairs={{0,8},{4,12},{8,16},{12,20},{16,24},{20,28},{1,9},{5,13},{9,17},{1... | collective-permute-start | bytes 1179656 | tf_op jit(solution)/shard_map/ppermute | solution.py:21
  1386.7 38.3 %collective-permute-start.1 = (bf16[1,256,768]{2,1,0:T(8,128)(2,1)}, bf16[1,256,768]{2,1,0:T(8,128)(2,1)}, u32[]{:S(2)}, u32[]{:S(2)}) collective-permute-start(bf16[1,256,768]{2,1,0:T(8,128)(2,1)} %bitcast.2), channel_id=1, source_target_pairs={{0,4},{4,8},{8,12},{12,16},{16,20},{20,24},{24,28},{1,5},{5,9},{9,... | collective-permute-start | bytes 1179656 | tf_op jit(solution)/shard_map/ppermute | solution.py:21
  1395.7 31.1 %collective-permute-start.2 = (bf16[1,256,768]{2,1,0:T(8,128)(2,1)}, bf16[1,256,768]{2,1,0:T(8,128)(2,1)}, u32[]{:S(2)}, u32[]{:S(2)}) collective-permute-start(bf16[1,256,768]{2,1,0:T(8,128)(2,1)} %bitcast.2), channel_id=1, source_target_pairs={{4,0},{8,4},{12,8},{16,12},{20,16},{24,20},{28,24},{5,1},{9,5},{13... | collective-permute-start | bytes 1179656 | tf_op jit(solution)/shard_map/ppermute | solution.py:21
  1398.9 29.8 %collective-permute-start.3 = (bf16[1,256,768]{2,1,0:T(8,128)(2,1)}, bf16[1,256,768]{2,1,0:T(8,128)(2,1)}, u32[]{:S(2)}, u32[]{:S(2)}) collective-permute-start(bf16[1,256,768]{2,1,0:T(8,128)(2,1)} %bitcast.2), channel_id=1, source_target_pairs={{8,0},{12,4},{16,8},{20,12},{24,16},{28,20},{9,1},{13,5},{17,9},{2... | collective-permute-start | bytes 1179656 | tf_op jit(solution)/shard_map/ppermute | solution.py:21
  1523.2 52.7 %all-to-all-start = ((bf16[8,2,16,768]{3,2,1,0:T(8,128)(2,1)}), bf16[8,2,16,768]{3,2,1,0:T(8,128)(2,1)}, u32[]{:S(2)}, u32[]{:S(2)}) async-start(bf16[8,2,16,768]{3,2,1,0:T(8,128)(2,1)} %copy.118), calls=%async_computation | async-start | bytes 786432 | tf_op jit(solution)/shard_map/all_to_all | solution.py:31
  1531.5 340.0 %reduce-scatter.8.cloned.1.call-start = ((), (), s32[]{:S(2)}) async-start(), calls=%async_computation.15 | async-start | bytes 1474560 | tf_op jit(solution)/shard_map/reduce_scatter | solution.py:491
  1551.5 320.1 %reduce-scatter.12.cloned.1.call-start = ((), (), s32[]{:S(2)}) async-start(), calls=%async_computation.17 | async-start | bytes 1474560 | tf_op jit(solution)/shard_map/reduce_scatter | solution.py:497
  1553.9 23.0 %copy-start.29 = (f32[16,768]{1,0:T(8,128)S(1)}, f32[16,768]{1,0:T(8,128)}, u32[]{:S(2)}) copy-start(f32[16,768]{1,0:T(8,128)} %copy-done.28) | copy-start | bytes 147460
  1554.0 23.0 %copy-start.43 = (f32[768]{0:T(1024)S(1)}, f32[768]{0:T(1024)}, u32[]{:S(2)}) copy-start(f32[768]{0:T(1024)} %copy-done.42) | copy-start | bytes 9220
  1554.0 12.2 collective-permute-start.12
  1555.3 18.2 collective-permute-start.13
  1559.8 14.7 collective-permute-start.14
  1561.1 13.4 collective-permute-start.15
  1577.0 35.2 %copy-start.40 = (f32[2,16,768]{2,1,0:T(8,128)}, f32[2,16,768]{2,1,0:T(8,128)S(1)}, u32[]{:S(2)}) copy-start(f32[2,16,768]{2,1,0:T(8,128)S(1)} %convert_reduce_fusion.2) | copy-start | bytes 294916
  1579.8 291.8 %reduce-scatter.10.cloned.1.call-start = ((), (), s32[]{:S(2)}) async-start(), calls=%async_computation.16 | async-start | bytes 1474560 | tf_op jit(solution)/shard_map/reduce_scatter | solution.py:494
  1584.9 12.9 collective-permute-start.10
  1586.2 11.7 collective-permute-start.11
  1590.7 12.2 collective-permute-start.8
  1592.0 19.9 collective-permute-start.9
  1615.0 256.5 %reduce-scatter.18.cloned.1.call-start = ((), (), s32[]{:S(2)}) async-start(), calls=%async_computation.20 | async-start | bytes 3932160 | tf_op jit(solution)/shard_map/reduce_scatter | solution.py:506
  1619.7 251.9 %reduce-scatter.16.cloned.1.call-start = ((), (), s32[]{:S(2)}) async-start(), calls=%async_computation.19 | async-start | bytes 3932160 | tf_op jit(solution)/shard_map/reduce_scatter | solution.py:503
  1623.8 247.9 %reduce-scatter.20.cloned.1.call-start = ((), (), s32[]{:S(2)}) async-start(), calls=%async_computation.21 | async-start | bytes 3932160 | tf_op jit(solution)/shard_map/reduce_scatter | solution.py:509
  (57 other events, 330.7 us)
Sparse Core Ops, SparseCore 0:
  9.6 20.2 all-gather.11
  31.4 17.4 all-gather.7
  50.5 17.4 all-gather.9
  69.4 17.4 all-gather.13
  88.2 28.4 all-gather.19
  118.2 28.4 all-gather.15
  148.3 28.4 all-gather.17
  1512.2 28.4 reduce-scatter.13
  1551.6 26.0 reduce-scatter.7
  1580.7 26.9 reduce-scatter.11
  1615.2 25.6 reduce-scatter.9
  1643.2 37.8 reduce-scatter.17
  1683.7 37.8 reduce-scatter.15
  1724.0 37.8 reduce-scatter.19
where the time goes:
time: 2180 us; the launch traced here: 2160 us
  local copies, waits for them, and re-layouts  1540 us (71%)
  blocking collectives  341 us (16%)
  matrix products  122 us (6%)
  starting transfers between devices  55.9 us (3%)
  other arithmetic  52.8 us (2%)
  waiting for transfers between devices  27.3 us (1%)
    gather x2, local copies, waits for them, and re-layouts, on_device(): jnp.take(near_table, near_index, axis=0)  1160 us
    psum x1, blocking collectives, on_device(): lax.psum((shared[0], shared[1], shared[2], shared[3], shared[4], shared[5...  280 us
    gather x2, local copies, waits for them, and re-layouts, on_device(): jnp.take(side_table, side_index, axis=0)  119 us
    rev x2, local copies, waits for them, and re-layouts, diagonal_sums(): flipped = jnp.pad(matrix[:, ::-1, :], ((0, 0), (0, 0), (0, row_count)))  115 us
    ppermute x16, starting transfers between devices, shifted(): return lax.ppermute(value, axis, pairs)  47 us
    unnamed x165, local copies, waits for them, and re-layouts  45.5 us
  transfers between devices with their start and end apart: 31, of which 6 were waited for; matrix products, arithmetic and copies ran while one was open for 77% of the time, Pallas kernels for 0%

commit v1 on v0

v1 whole, which is shorter than its diff:
```python
import jax
import jax.numpy as jnp
from jax import lax
from jax.experimental import pallas as pl
from jax.experimental.pallas import tpu as pltpu
from jax.sharding import PartitionSpec as P

H = 12
HD = 64
NB = 32
GB = 16
HALF = 512
LANES = 128
PAIRS = H * HD // LANES

EPS = 1e-06
NEG = -1e30
HIGHEST = lax.Precision.HIGHEST
VMEM_LIMIT = 60 << 20


def shifted(value, axis, by):
    length = lax.axis_size(axis)
    pairs = [(i, i + by) for i in range(length) if 0 <= i + by < length]
    return lax.ppermute(value, axis, pairs)


def dot_nn(left, right):
    return lax.dot_general(
        left, right, (((1,), (0,)), ((), ())), preferred_element_type=jnp.float32
    )


def dot_nt(left, right):
    return lax.dot_general(
        left, right, (((1,), (1,)), ((), ())), preferred_element_type=jnp.float32
    )


def dot_tn(left, right):
    return lax.dot_general(
        left, right, (((0,), (0,)), ((), ())), preferred_element_type=jnp.float32
    )


def rms_scale(values):
    return lax.rsqrt(jnp.mean(values * values, axis=-1, keepdims=True) + EPS)


def norm_back(upstream, normed_val, row_scale, gain_row):
    scaled = upstream * gain_row
    return row_scale * (scaled - normed_val * jnp.mean(scaled * normed_val, axis=-1, keepdims=True))


def head_mask(head):
    lane = lax.broadcasted_iota(jnp.int32, (1, LANES), 1)
    own = (lane < HD) if head == 0 else (lane >= HD)
    return own.astype(jnp.float32)


def fill_offsets(base_ref, head, table_ref):
    width = table_ref.shape[1]
    base = jnp.broadcast_to(base_ref[0, head : head + 1, :], (8, width))
    base = pltpu.roll(base, 0, 1, stride=1, stride_axis=0)
    for group in range(LANES // 8):
        table_ref[group * 8 : group * 8 + 8, :] = (
            pltpu.roll(base, group * 8, 1) if group else base
        )


def score_rows(score_ref, table_ref, far_ref, head, half, step, near_len):
    row = pl.multiple_of(half * LANES + step * GB, GB)
    start = LANES if half == 0 else 0
    bias = table_ref[pl.ds(pl.multiple_of(step * GB, GB), GB), start : start + near_len]
    near = score_ref[pl.ds(row, GB), :near_len] + bias
    far = score_ref[pl.ds(row, GB), near_len:] + far_ref[
        0, head, pl.ds(half * (LANES // GB) + step, 1), :
    ]
    return row, near, far


def forward_kernel(
    q_ref, k_ref, v_ref, q_label_ref, k_label_ref, base_ref, far_ref,
    out_ref, log_ref,
    table_ref, score_ref, prob_ref, total_ref,
):
    rows = q_ref.shape[0]
    near_len = table_ref.shape[1] - LANES
    keys = jnp.concatenate([k_ref[...], k_label_ref[...]], axis=1)
    out = None
    logs = None
    for head in range(2):
        mask = head_mask(head)
        query = jnp.concatenate(
            [q_ref[...] * mask.astype(jnp.bfloat16), q_label_ref[...]], axis=1
        )
        score_ref[...] = dot_nt(query, keys)
        fill_offsets(base_ref, head, table_ref)
        for half in range(rows // LANES):

            def body(step, carry, half=half, head=head):
                row, near, far = score_rows(
                    score_ref, table_ref, far_ref, head, half, step, near_len
                )
                peak = jnp.maximum(
                    jnp.max(near, axis=1, keepdims=True), jnp.max(far, axis=1, keepdims=True)
                )
                near = jnp.exp(near - peak)
                far = jnp.exp(far - peak)
                total = jnp.sum(near, axis=1, keepdims=True) + jnp.sum(far, axis=1, keepdims=True)
                prob_ref[pl.ds(row, GB), :near_len] = near.astype(jnp.bfloat16)
                prob_ref[pl.ds(row, GB), near_len:] = far.astype(jnp.bfloat16)
                total_ref[0, pl.ds(row, GB), :] = jnp.broadcast_to(total, (GB, LANES))
                total_ref[1, pl.ds(row, GB), :] = jnp.broadcast_to(
                    peak + jnp.log(total), (GB, LANES)
                )
                return carry

            lax.fori_loop(0, LANES // GB, body, 0, unroll=2)
        mixed = dot_nn(prob_ref[...], v_ref[...]) / total_ref[0] * mask
        out = mixed if out is None else out + mixed
        part = total_ref[1] * mask
        logs = part if logs is None else logs + part
    out_ref[...] = out.astype(jnp.bfloat16)
    log_ref[0] = logs


def backward_kernel(
    q_ref, k_ref, v_ref, g_ref, o_ref, log_ref, q_label_ref, k_label_ref, base_ref, far_ref,
    dq_ref, dk_ref, dv_ref, diag_ref, dfar_ref,
    table_ref, score_ref, dprob_ref, prob_ref, delta_ref, fold_ref, col_ref, q_two, g_two,
):
    rows = q_ref.shape[0]
    near_len = table_ref.shape[1] - LANES
    keys = jnp.concatenate([k_ref[...], k_label_ref[...]], axis=1)
    weighted = g_ref[...].astype(jnp.float32) * o_ref[...].astype(jnp.float32)
    for head in range(2):
        mask = head_mask(head)
        mask_low = mask.astype(jnp.bfloat16)
        own_q = q_ref[...] * mask_low
        own_g = g_ref[...] * mask_low
        q_two[head * rows : (head + 1) * rows, :] = own_q
        g_two[head * rows : (head + 1) * rows, :] = own_g
        query = jnp.concatenate([own_q, q_label_ref[...]], axis=1)
        score_ref[...] = dot_nt(query, keys)
        dprob_ref[...] = dot_nt(own_g, v_ref[...])
        fill_offsets(base_ref, head, table_ref)
        col_ref[0] = jnp.broadcast_to(
            jnp.sum(weighted * mask, axis=1, keepdims=True), (rows, LANES)
        )
        col_ref[1] = jnp.broadcast_to(
            log_ref[0, :, head * HD : head * HD + 1], (rows, LANES)
        )
        for half in range(rows // LANES):

            def body(step, carry, half=half, head=head):
                row, near, far = score_rows(
                    score_ref, table_ref, far_ref, head, half, step, near_len
                )
                center = col_ref[0, pl.ds(row, GB), 0:1]
                logs = col_ref[1, pl.ds(row, GB), 0:1]
                to_row = pl.multiple_of(head * rows + row, GB)
                near = jnp.exp(near - logs)
                far = jnp.exp(far - logs)
                prob_ref[pl.ds(to_row, GB), :near_len] = near.astype(jnp.bfloat16)
                prob_ref[pl.ds(to_row, GB), near_len:] = far.astype(jnp.bfloat16)
                near = near * (dprob_ref[pl.ds(row, GB), :near_len] - center)
                far = far * (dprob_ref[pl.ds(row, GB), near_len:] - center)
                delta_ref[pl.ds(to_row, GB), :near_len] = near.astype(jnp.bfloat16)
                delta_ref[pl.ds(to_row, GB), near_len:] = far.astype(jnp.bfloat16)
                at = pl.ds(pl.multiple_of(step * GB, GB), GB)
                if half == 0:
                    fold_ref[at, :LANES] = jnp.zeros((GB, LANES), jnp.float32)
                    fold_ref[at, LANES:] = near
                else:
                    fold_ref[at, :near_len] += near
                dfar_ref[0, head, pl.ds(half * (LANES // GB) + step, 1), :] = jnp.sum(
                    far, axis=0, keepdims=True
                )
                return carry

            lax.fori_loop(0, LANES // GB, body, 0, unroll=2)
        diag = fold_ref[0:8, :]
        width = table_ref.shape[1]
        for group in range(1, LANES // 8):
            diag = diag + pltpu.roll(fold_ref[group * 8 : group * 8 + 8, :], width - group * 8, 1)
        diag_ref[0, head] = diag
    low = dot_nn(delta_ref[:rows, :], k_ref[...]) * head_mask(0)
    high = dot_nn(delta_ref[rows:, :], k_ref[...]) * head_mask(1)
    dq_ref[...] = (low + high).astype(jnp.bfloat16)
    dk_ref[...] = dot_tn(q_two[...], delta_ref[...]).T.astype(jnp.bfloat16)
    dv_ref[...] = dot_tn(g_two[...], prob_ref[...]).T.astype(jnp.bfloat16)


def attention_specs(rows, total, width, far_len):
    col = lambda p: (0, p)
    return dict(
        q=pl.BlockSpec((rows, LANES), col),
        k=pl.BlockSpec((total, LANES), col),
        q_label=pl.BlockSpec((rows, LANES), lambda p: (0, 0)),
        k_label=pl.BlockSpec((total, LANES), lambda p: (0, 0)),
        base=pl.BlockSpec((1, 2, width), lambda p: (p, 0, 0)),
        far=pl.BlockSpec((1, 2, rows // GB, far_len), lambda p: (p, 0, 0, 0)),
        log=pl.BlockSpec((1, rows, LANES), lambda p: (p, 0, 0)),
        diag=pl.BlockSpec((1, 2, 8, width), lambda p: (p, 0, 0, 0)),
    )


def attention_forward(q, k, v, q_label, k_label, base, far):
    rows, total, width, far_len = q.shape[0], k.shape[0], base.shape[2], far.shape[3]
    s = attention_specs(rows, total, width, far_len)
    return pl.pallas_call(
        forward_kernel,
        grid=(PAIRS,),
        in_specs=[s["q"], s["k"], s["k"], s["q_label"], s["k_label"], s["base"], s["far"]],
        out_specs=[s["q"], s["log"]],
        out_shape=[
            jax.ShapeDtypeStruct((rows, PAIRS * LANES), jnp.bfloat16),
            jax.ShapeDtypeStruct((PAIRS, rows, LANES), jnp.float32),
        ],
        scratch_shapes=[
            pltpu.VMEM((LANES, width), jnp.float32),
            pltpu.VMEM((rows, total), jnp.float32),
            pltpu.VMEM((rows, total), jnp.bfloat16),
            pltpu.VMEM((2, rows, LANES), jnp.float32),
        ],
        compiler_params=pltpu.CompilerParams(vmem_limit_bytes=VMEM_LIMIT),
        name="attention_forward",
    )(q, k, v, q_label, k_label, base, far)


def attention_backward(q, k, v, g, o, logs, q_label, k_label, base, far):
    rows, total, width, far_len = q.shape[0], k.shape[0], base.shape[2], far.shape[3]
    s = attention_specs(rows, total, width, far_len)
    return pl.pallas_call(
        backward_kernel,
        grid=(PAIRS,),
        in_specs=[
            s["q"], s["k"], s["k"], s["q"], s["q"], s["log"],
            s["q_label"], s["k_label"], s["base"], s["far"],
        ],
        out_specs=[s["q"], s["k"], s["k"], s["diag"], s["far"]],
        out_shape=[
            jax.ShapeDtypeStruct((rows, PAIRS * LANES), jnp.bfloat16),
            jax.ShapeDtypeStruct((total, PAIRS * LANES), jnp.bfloat16),
            jax.ShapeDtypeStruct((total, PAIRS * LANES), jnp.bfloat16),
            jax.ShapeDtypeStruct((PAIRS, 2, 8, width), jnp.float32),
            jax.ShapeDtypeStruct((PAIRS, 2, rows // GB, far_len), jnp.float32),
        ],
        scratch_shapes=[
            pltpu.VMEM((LANES, width), jnp.float32),
            pltpu.VMEM((rows, total), jnp.float32),
            pltpu.VMEM((rows, total), jnp.float32),
            pltpu.VMEM((2 * rows, total), jnp.bfloat16),
            pltpu.VMEM((2 * rows, total), jnp.bfloat16),
            pltpu.VMEM((LANES, width), jnp.float32),
            pltpu.VMEM((2, rows, LANES), jnp.float32),
            pltpu.VMEM((2 * rows, LANES), jnp.bfloat16),
            pltpu.VMEM((2 * rows, LANES), jnp.bfloat16),
        ],
        compiler_params=pltpu.CompilerParams(vmem_limit_bytes=VMEM_LIMIT),
        name="attention_backward",
    )(q, k, v, g, o, logs, q_label, k_label, base, far)


def on_device(
    hidden, cotangent, query_proj, key_proj, value_proj, out_proj, gate_proj, up_proj,
    down_proj, first_gain, second_gain, global_gain, local_bias, side_bias,
    segments, local_buckets, global_buckets,
):
    x_own = hidden[0]
    cot = cotangent[0]
    rows, width = x_own.shape
    cycle_size = lax.axis_size("ctx")
    cycle_index = lax.axis_index("ctx")
    first_row = cycle_index * rows
    far_len = rows * cycle_size // GB
    own_blocks = rows // GB
    reach = HALF // rows
    near_len = rows + 2 * HALF

    left = [shifted(x_own, "ctx", d) for d in range(reach, 0, -1)]
    right = [shifted(x_own, "ctx", -d) for d in range(1, reach + 1)]
    window = jnp.concatenate(left + [x_own] + right, axis=0)

    gather = lambda a: lax.all_gather(a, "shard", axis=0, tiled=True)
    w_query, w_key, w_value, w_out = map(gather, (query_proj, key_proj, value_proj, out_proj))
    w_gate, w_up, w_down = map(gather, (gate_proj, up_proj, down_proj))
    small = jnp.concatenate(
        [first_gain, second_gain, global_gain, local_bias.reshape(-1), side_bias.reshape(-1)]
    )
    small = gather(small[None])
    cut = first_gain.shape[0]
    gain_one = small[:, :cut].reshape(-1).astype(jnp.float32)
    gain_two = small[:, cut : 2 * cut].reshape(-1).astype(jnp.float32)
    gain_side = small[:, 2 * cut : 3 * cut].reshape(-1).astype(jnp.float32)
    tab = local_bias.size
    near_tab = small[:, 3 * cut : 3 * cut + tab].reshape(NB, H)
    side_tab = small[:, 3 * cut + tab :].reshape(NB, H)

    bucket_iota = jnp.arange(NB, dtype=jnp.int32)[None, :]
    onehot_near = (local_buckets[:, None] == bucket_iota).astype(jnp.bfloat16)
    near_row = lax.dot_general(
        near_tab, onehot_near, (((0,), (1,)), ((), ())), preferred_element_type=jnp.float32
    )
    table_width = near_len + LANES
    base = jnp.pad(
        near_row,
        ((0, 0), (LANES + 1, table_width - LANES - 1 - near_row.shape[1])),
        constant_values=NEG,
    ).reshape(PAIRS, 2, table_width)
    far_start = far_len - own_blocks - cycle_index * own_blocks
    bucket_slice = lax.dynamic_slice_in_dim(global_buckets, far_start, far_len + own_blocks - 1, 0)
    onehot_side = (bucket_slice[:, None] == bucket_iota).astype(jnp.bfloat16)
    side_row = lax.dot_general(
        side_tab, onehot_side, (((0,), (1,)), ((), ())), preferred_element_type=jnp.float32
    )
    far = jnp.stack(
        [side_row[:, own_blocks - 1 - r : own_blocks - 1 - r + far_len] for r in range(own_blocks)],
        axis=1,
    ).reshape(PAIRS, 2, own_blocks, far_len)
    labels = segments[0]
    label_iota = jnp.arange(LANES, dtype=jnp.int32)[None, :]
    label_query = lax.dynamic_slice_in_dim(labels, first_row, rows, 0)
    label_pad = jnp.pad(labels, (HALF, HALF), constant_values=-1)
    label_window = lax.dynamic_slice_in_dim(label_pad, first_row, near_len, 0)
    label_keys = jnp.concatenate([label_window, labels[::GB]])
    q_label = (label_query[:, None] == label_iota).astype(jnp.bfloat16)
    k_label = jnp.where(label_keys[:, None] == label_iota, 0.0, NEG).astype(jnp.bfloat16)

    wide = window.astype(jnp.float32)
    scale_wide = rms_scale(wide)
    normed_wide = ((wide * scale_wide) * gain_one).astype(jnp.bfloat16)
    inputs = x_own.astype(jnp.float32)
    scale_one = rms_scale(inputs)
    normed_one = inputs * scale_one
    normed = (normed_one * gain_one).astype(jnp.bfloat16)
    block_sums = jnp.sum(normed.astype(jnp.float32).reshape(own_blocks, GB, width), axis=1)
    scale_side = rms_scale(block_sums)
    normed_side = block_sums * scale_side
    side_rows = (normed_side * gain_side).astype(jnp.bfloat16)
    all_rows = lax.all_gather(side_rows, "ctx", axis=0, tiled=True)
    key_rows = jnp.concatenate([normed_wide, all_rows], axis=0)
    queries = dot_nn(normed, w_query).astype(jnp.bfloat16)
    keys = dot_nn(key_rows, w_key).astype(jnp.bfloat16)
    values = dot_nn(key_rows, w_value).astype(jnp.bfloat16)
    attended, logs = attention_forward(queries, keys, values, q_label, k_label, base, far)
    middle = inputs + dot_nn(attended, w_out)
    scale_two = rms_scale(middle)
    normed_two = middle * scale_two
    ffn_in = (normed_two * gain_two).astype(jnp.bfloat16)
    gate_pre = dot_nn(ffn_in, w_gate)
    up_pre = dot_nn(ffn_in, w_up)
    gelu_out, gelu_pull = jax.vjp(lambda v: jax.nn.gelu(v, approximate=True), gate_pre)
    product = (gelu_out * up_pre).astype(jnp.bfloat16)
    outputs = (middle + dot_nn(product, w_down)).astype(jnp.bfloat16)

    down_grad = dot_tn(product, cot)
    product_grad = dot_nt(cot, w_down)
    gate_delta = gelu_pull(product_grad * up_pre)[0].astype(jnp.bfloat16)
    up_delta = (product_grad * gelu_out).astype(jnp.bfloat16)
    gate_grad = dot_tn(ffn_in, gate_delta)
    up_grad = dot_tn(ffn_in, up_delta)
    ffn_back = dot_nt(gate_delta, w_gate) + dot_nt(up_delta, w_up)
    second_part = jnp.sum(ffn_back * normed_two, axis=0)
    middle_grad = cot.astype(jnp.float32) + norm_back(ffn_back, normed_two, scale_two, gain_two)
    mixed_grad = middle_grad.astype(jnp.bfloat16)
    out_grad = dot_tn(attended, mixed_grad)
    attended_grad = dot_nt(mixed_grad, w_out).astype(jnp.bfloat16)

    dq, dk, dv, diag, dfar = attention_backward(
        queries, keys, values, attended_grad, attended, logs, q_label, k_label, base, far
    )
    query_grad = dot_tn(normed, dq)
    key_grad = dot_tn(key_rows, dk)
    value_grad = dot_tn(key_rows, dv)
    key_back = dot_nt(dk, w_key) + dot_nt(dv, w_value)
    own_start = reach * rows
    normed_back = dot_nt(dq, w_query) + key_back[own_start : own_start + rows]
    back_low = key_back.astype(jnp.bfloat16)
    for distance in range(1, reach + 1):
        for direction in (1, -1):
            at = (reach - direction * distance) * rows
            normed_back = normed_back + shifted(
                back_low[at : at + rows], "ctx", -direction * distance
            ).astype(jnp.float32)
    side_blocks = back_low[near_len:].reshape(cycle_size, own_blocks, width)
    side_blocks = lax.all_to_all(side_blocks, "ctx", 0, 0, tiled=True)
    side_back = jnp.sum(side_blocks.astype(jnp.float32), axis=0)
    global_part = jnp.sum(side_back * normed_side, axis=0)
    sums_grad = norm_back(side_back, normed_side, scale_side, gain_side)
    normed_back = (
        normed_back.reshape(own_blocks, GB, width) + sums_grad[:, None, :]
    ).reshape(rows, width)
    first_part = jnp.sum(normed_back * normed_one, axis=0)
    hidden_grad = (
        middle_grad + norm_back(normed_back, normed_one, scale_one, gain_one)
    ).astype(jnp.bfloat16)

    diag = diag.reshape(H, 8, table_width)
    near_sum = diag[:, 0]
    for r in range(1, 8):
        near_sum = near_sum + jnp.roll(diag[:, r], -r, axis=1)
    near_sum = near_sum[:, LANES + 1 : LANES + 2 * HALF]
    local_part = lax.dot_general(
        onehot_near.astype(jnp.float32), near_sum, (((0,), (1,)), ((), ())), precision=HIGHEST
    )
    dfar = dfar.reshape(H, own_blocks, far_len)
    side_sum = sum(
        jnp.pad(dfar[:, r], ((0, 0), (own_blocks - 1 - r, r))) for r in range(own_blocks)
    )
    side_part = lax.dot_general(
        onehot_side.astype(jnp.float32), side_sum, (((0,), (1,)), ((), ())), precision=HIGHEST
    )

    scatter = lambda a: lax.psum_scatter(
        a.astype(jnp.bfloat16), "shard", scatter_dimension=0, tiled=True
    )
    big = [scatter(a) for a in (query_grad, key_grad, value_grad, out_grad, gate_grad, up_grad, down_grad)]
    big = [lax.psum(a, "ctx").astype(jnp.float32) for a in big]
    tiny = jnp.concatenate(
        [a.reshape(-1) for a in (first_part, second_part, global_part, local_part, side_part)]
    )
    tiny = lax.psum(tiny.reshape(-1, LANES), ("ctx", "shard")).reshape(-1)
    shard = lax.axis_index("shard")
    done, at = [], 0
    for a in (first_part, second_part, global_part, local_part, side_part):
        whole = tiny[at : at + a.size].reshape(a.shape)
        at += a.size
        part = a.shape[0] // lax.axis_size("shard")
        done.append(lax.dynamic_slice_in_dim(whole, shard * part, part, 0))
    return (outputs[None], hidden_grad[None], *big, *done)


def solution(mesh):
    tokens = P("shard", "ctx", None)
    weight = P("shard", None)
    gain = P("shard")
    return jax.shard_map(
        on_device,
        mesh=mesh,
        in_specs=(tokens, tokens) + (weight,) * 7 + (gain,) * 3 + (weight,) * 3 + (P(), P()),
        out_specs=(tokens, tokens) + (weight,) * 7 + (gain,) * 3 + (weight,) * 2,
        check_vma=False,
    )
```

time: 2180 us -> 611 us (0.28)
  local copies, waits for them, and re-layouts: 1540 us -> 22.6 us
  waiting for transfers between devices: 27.3 us -> 310 us
  blocking collectives: 341 us -> 79.6 us
  Pallas kernels: 0 us -> 58.9 us
  matrix products: 122 us -> 78.9 us
  other arithmetic: 52.8 us -> 15.6 us
  starting transfers between devices: 55.9 us -> 29.8 us
    gather x4 -> x0, local copies, waits for them, and re-layouts: 1280 us -> none  [the longest x2 1160 us: on_device(): jnp.take(near_table, near_index, axis=0)]
    psum x1, blocking collectives: 280 us -> 40.3 us  [on_device(): tiny = lax.psum(tiny.reshape(-1, LANES), ('ctx', 'shard')).reshape(-1)]
    reduce_scatter x7, waiting for transfers between devices: 0.06 us -> 166 us  [on_device(): lax.psum_scatter(a.astype(jnp.bfloat16), 'shard', scatter_dimension=0, ti...]
    rev x2 -> x0, local copies, waits for them, and re-layouts: 115 us -> none  [diagonal_sums(): flipped = jnp.pad(matrix[:, ::-1, :], ((0, 0), (0, 0), (0, row_count)))]
    pallas_call x0 -> x2, Pallas kernels: none -> 58.9 us  [the longest x1 30.4 us: attention_forward(): pl.pallas_call(forward_kernel, grid=(PAIRS,), in_specs=[s['q'], s['k'], s...]
    all_gather x7, waiting for transfers between devices: 0.07 us -> 53.8 us  [on_device(): gather = lambda a: lax.all_gather(a, 'shard', axis=0, tiled=True)]
    psum x0 -> x1, waiting for transfers between devices: none -> 45.7 us  [on_device(): big = [lax.psum(a, 'ctx').astype(jnp.float32) for a in big]]
    dot_general x43 -> x25, matrix products: 122 us -> 78.9 us  [the longest x7 26.3 us: dot_nn(): lax.dot_general(left, right, (((1,), (0,)), ((), ())), preferred_element_...]
  transfers between devices with their start and end apart: 31 -> 24, of which waited for: 6 -> 10; matrix products, arithmetic and copies ran while one was open for 77% -> 15% of each run, Pallas kernels for 0% -> 10%
where the time goes in v1:
time: 611 us; the launch traced here: 610 us
  waiting for transfers between devices  310 us (51%)
  blocking collectives  79.6 us (13%)
  matrix products  78.9 us (13%)
  Pallas kernels  58.9 us (10%)
  starting transfers between devices  29.8 us (5%)
  local copies, waits for them, and re-layouts  22.6 us (4%)
  other arithmetic  15.6 us (3%)
  between operations  14.9 us (2%)
    reduce_scatter x7, waiting for transfers between devices, on_device(): lax.psum_scatter(a.astype(jnp.bfloat16), 'shard', scatter_dimension=0, ti...  166 us
    all_gather x7, waiting for transfers between devices, on_device(): gather = lambda a: lax.all_gather(a, 'shard', axis=0, tiled=True)  53.8 us
    psum x1, waiting for transfers between devices, on_device(): big = [lax.psum(a, 'ctx').astype(jnp.float32) for a in big]  45.7 us
    psum x1, blocking collectives, on_device(): tiny = lax.psum(tiny.reshape(-1, LANES), ('ctx', 'shard')).reshape(-1)  40.3 us
    all_to_all x1, waiting for transfers between devices, on_device(): side_blocks = lax.all_to_all(side_blocks, 'ctx', 0, 0, tiled=True)  39.8 us
    all_gather x1, blocking collectives, on_device(): all_rows = lax.all_gather(side_rows, 'ctx', axis=0, tiled=True)  33.9 us
    pallas_call x1, Pallas kernels, attention_forward(): pl.pallas_call(forward_kernel, grid=(PAIRS,), in_specs=[s['q'], s['k'], s...  30.4 us
    pallas_call x1, Pallas kernels, attention_backward(): pl.pallas_call(backward_kernel, grid=(PAIRS,), in_specs=[s['q'], s['k'],...  28.5 us
  transfers between devices with their start and end apart: 24, of which 10 were waited for; matrix products, arithmetic and copies ran while one was open for 15% of the time, Pallas kernels for 10%

profile of v1, /device:TPU:0, one launch (start us, length us, event | category | flops | bytes accessed | tf_op | source)
XLA Modules:
  0.0 609.8 jit_solution(3681075752804260308)
XLA Ops:
  11.3 5.0 collective-permute-start
  16.3 3.4 collective-permute-start.1
  19.7 1.3 collective-permute-start.2
  21.0 1.3 collective-permute-start.3
  22.7 5.4 all-gather.1
  32.5 1.4 stack.67.far_ref
  33.9 33.9 %all_gather.29 = bf16[128,768]{1,0:T(8,128)(2,1)S(1)} all-gather(bf16[16,768]{1,0:T(8,128)(2,1)S(1)} %multiply_convert_fusion.3), channel_id=1, replica_groups=mesh['ctx'=8,'shard'=4] {'ctx'}, dimensions={0}, use_global_device_ids=true | all-gather | bytes 221184 | tf_op jit(solution)/shard_map/all_gather | solution.py:342
  69.7 3.2 convolution_convert_fusion.10.q_ref
  73.0 4.5 convolution_convert_fusion.3.v_ref
  77.5 4.5 convolution_convert_fusion.4.k_ref
  81.9 30.4 %attention_forward.1 = (bf16[256,768]{1,0:T(8,128)(2,1)}, f32[6,256,128]{2,1,0:T(8,128)}) custom-call(bf16[256,768]{1,0:T(8,128)(2,1)} %convolution_convert_fusion.10.q_ref, bf16[1408,768]{1,0:T(8,128)(2,1)} %convolution_convert_fusion.4.k_ref, bf16[1408,768]{1,0:T(8,128)(2,1)} %convolution_convert_fusion.3.v_ref, bf16[256,128]{1,0:T(8,128)(2,1)} %fusion.38.q_label_ref, ...), custom_call_target="tpu_custom_call" | custom-call | tf_op jit(solution)/shard_map/attention_forward/pallas_call | solution.py:212
  112.4 2.0 multiply_reduce_fusion.2
  114.5 2.2 all-gather.18.cloned.1.call-done
  116.8 4.2 fusion.103
  121.0 25.8 %all-gather.20.cloned.1.call-done = bf16[768,2048]{1,0:T(8,128)(2,1)} async-done(((bf16[192,2048]{1,0:T(8,128)(2,1)}), bf16[768,2048]{1,0:T(8,128)(2,1)}) %all-gather.20.cloned.1.call-update) | async-done | bytes 3145744 | tf_op jit(solution)/shard_map/all_gather | solution.py:286
  146.7 4.3 fusion.104
  151.1 25.8 %all-gather.22.cloned.1.call-done = bf16[2048,768]{1,0:T(8,128)(2,1)} async-done(((bf16[512,768]{1,0:T(8,128)(2,1)}), bf16[2048,768]{1,0:T(8,128)(2,1)}) %all-gather.22.cloned.1.call-update) | async-done | bytes 3145744 | tf_op jit(solution)/shard_map/all_gather | solution.py:286
  176.8 6.5 %multiply_convert_fusion = (bf16[256,2048]{1,0:T(8,128)(2,1)S(1)}, bf16[256,2048]{1,0:T(8,128)(2,1)S(1)}, bf16[256,2048]{1,0:T(8,128)(2,1)}) fusion(f32[256,2048]{1,0:T(8,128)} %fusion.103, f32[256,2048]{1,0:T(8,128)} %fusion.104, bf16[2048,768]{1,0:T(8,128)(2,1)} %all-gather.22.cloned.1.call-done, bf16[1,256,768]{2,1,0:T(8,128)(2,1)S(1)} %copy-done.9), kind=kOutput, calls=%fused_computation.21 | convolution fusion | flops 818937856 | bytes 10878976 | tf_op jit(solution)/shard_map/dot_general | solution.py:35
  184.7 1.3 copy-done.1
  186.0 1.7 multiply_reduce_fusion
  188.7 1.5 convolution_convert_fusion.5
  191.6 28.5 %attention_backward.1 = (bf16[256,768]{1,0:T(8,128)(2,1)}, bf16[1408,768]{1,0:T(8,128)(2,1)}, bf16[1408,768]{1,0:T(8,128)(2,1)}, f32[6,2,8,1408]{3,2,1,0:T(8,128)}, f32[6,2,16,128]{3,2,1,0:T(8,128)}) custom-call(bf16[256,768]{1,0:T(8,128)(2,1)} %convolution_convert_fusion.10.q_ref, bf16[1408,768]{1,0:T(8,128)(2,1)} %convolution_convert_fusion.4.k_ref, ...), custom_call_target="tpu_custom_call" | custom-call | tf_op jit(solution)/shard_map/attention_backward/pallas_call | solution.py:235
  220.0 5.3 convolution_convert_fusion.7
  225.4 5.3 convolution_convert_fusion.6
  230.8 1.6 convolution_convert_fusion.8
  232.5 4.0 convolution_convert_fusion.2
  237.7 2.8 convolution_convert_fusion.1
  241.9 2.8 convolution_convert_fusion
  253.3 1.4 reshape.270
  255.7 1.6 fusion.32
  257.4 5.8 fusion.106
  263.2 16.5 %reduce-scatter.12.cloned.1.call-done = bf16[192,768]{1,0:T(8,128)(2,1)} async-done(((bf16[768,768]{1,0:T(8,128)(2,1)}), bf16[192,768]{1,0:T(8,128)(2,1)}) %reduce-scatter.12.cloned.1.call-update) | async-done | bytes 294928 | tf_op jit(solution)/shard_map/reduce_scatter | solution.py:416
  279.7 28.8 %reduce-scatter.8.cloned.1.call-done = bf16[192,768]{1,0:T(8,128)(2,1)} async-done(((bf16[768,768]{1,0:T(8,128)(2,1)}), bf16[192,768]{1,0:T(8,128)(2,1)}) %reduce-scatter.8.cloned.1.call-update) | async-done | bytes 294928 | tf_op jit(solution)/shard_map/reduce_scatter | solution.py:416
  308.5 40.3 %reduce-scatter.16.cloned.1.call-done = bf16[192,2048]{1,0:T(8,128)(2,1)} async-done(((bf16[768,2048]{1,0:T(8,128)(2,1)}), bf16[192,2048]{1,0:T(8,128)(2,1)}) %reduce-scatter.16.cloned.1.call-update) | async-done | bytes 786448 | tf_op jit(solution)/shard_map/reduce_scatter | solution.py:416
  348.8 40.5 %reduce-scatter.18.cloned.1.call-done = bf16[192,2048]{1,0:T(8,128)(2,1)} async-done(((bf16[768,2048]{1,0:T(8,128)(2,1)}), bf16[192,2048]{1,0:T(8,128)(2,1)}) %reduce-scatter.18.cloned.1.call-update) | async-done | bytes 786448 | tf_op jit(solution)/shard_map/reduce_scatter | solution.py:416
  389.3 40.3 %reduce-scatter.20.cloned.1.call-done = bf16[512,768]{1,0:T(8,128)(2,1)} async-done(((bf16[2048,768]{1,0:T(8,128)(2,1)}), bf16[512,768]{1,0:T(8,128)(2,1)}) %reduce-scatter.20.cloned.1.call-update) | async-done | bytes 786448 | tf_op jit(solution)/shard_map/reduce_scatter | solution.py:416
  429.6 7.1 %fusion.102 = (bf16[1408,768]{1,0:T(8,128)(2,1)S(1)}, f32[1408,768]{1,0:T(8,128)}) fusion(f32[1408,768]{1,0:T(8,128)} %fusion.106, bf16[1408,768]{1,0:T(8,128)(2,1)} %get-tuple-element.25, bf16[768,768]{1,0:T(8,128)(2,1)} %all-gather.14.cloned.1.call-done), kind=kOutput, calls=%fused_computation.203 | convolution fusion | flops 1663107072 | bytes 14155776 | tf_op jit(solution)/shard_map/dot_general | solution.py:35
  438.6 1.3 collective-permute-start.4
  439.9 5.3 collective-permute-start.5
  446.5 5.3 collective-permute-start.7
  451.9 4.7 all-to-all-start
  456.6 3.7 fusion.11
  460.3 39.8 %all-to-all-done = bf16[8,16,768]{2,1,0:T(8,128)(2,1)} async-done(((bf16[8,16,768]{2,1,0:T(8,128)(2,1)}), bf16[8,16,768]{2,1,0:T(8,128)(2,1)}, u32[]{:S(2)}, u32[]{:S(2)}) %all-to-all-start) | async-done | bytes 196640 | tf_op jit(solution)/shard_map/all_to_all | solution.py:388
  501.5 2.8 fusion.22
  504.4 40.3 %psum.63 = f32[24,128]{1,0:T(8,128)S(1)} all-reduce(f32[24,128]{1,0:T(8,128)S(1)} %bitcast.143), channel_id=1, replica_groups=mesh['ctx'=8,'shard'=4] {'ctx','shard'}, use_global_device_ids=true, to_apply=%region_26.27 | all-reduce | flops 3072 | bytes 24576 | tf_op jit(solution)/shard_map/psum | solution.py:424
  549.0 45.7 %all-reduce.21.cloned.1.call-done = (bf16[192,768]{1,0:T(8,128)(2,1)}, bf16[192,768]{1,0:T(8,128)(2,1)}, bf16[192,768]{1,0:T(8,128)(2,1)}, bf16[192,768]{1,0:T(8...) async-done(((bf16[192,768]{1,0:T(8,128)(2,1)}, bf16[192,768]{1,0:T(8,128)(2,1)}, bf16[192,768]{1,0:T(8,128)(2,1)}, ...) | async-done | bytes 3538960 | tf_op jit(solution)/shard_map/psum | solution.py:420
  594.7 2.6 convert_element_type.249
  597.3 1.3 convert_element_type.251
  (258 shorter events, 39.9 us)
Async XLA Ops:
  7.2 15.2 %copy-start.39 = (bf16[8,12]{1,0:T(8,128)(2,1)S(1)}, bf16[8,12]{1,0:T(8,128)(2,1)}, u32[]{:S(2)}) copy-start(bf16[8,12]{1,0:T(8,128)(2,1)} %param.29) | copy-start | bytes 580
  7.2 15.3 %copy-start.40 = (bf16[8,12]{1,0:T(8,128)(2,1)S(1)}, bf16[8,12]{1,0:T(8,128)(2,1)}, u32[]{:S(2)}) copy-start(bf16[8,12]{1,0:T(8,128)(2,1)} %param.30) | copy-start | bytes 580
  7.2 15.4 %copy-start.44 = (bf16[192]{0:T(256)(128)(2,1)S(1)}, bf16[192]{0:T(256)(128)(2,1)}, u32[]{:S(2)}) copy-start(bf16[192]{0:T(256)(128)(2,1)} %param.26) | copy-start | bytes 1156
  7.2 15.4 %copy-start.45 = (bf16[192]{0:T(256)(128)(2,1)S(1)}, bf16[192]{0:T(256)(128)(2,1)}, u32[]{:S(2)}) copy-start(bf16[192]{0:T(256)(128)(2,1)} %param.27) | copy-start | bytes 1156
  7.2 15.4 %copy-start.46 = (bf16[192]{0:T(256)(128)(2,1)S(1)}, bf16[192]{0:T(256)(128)(2,1)}, u32[]{:S(2)}) copy-start(bf16[192]{0:T(256)(128)(2,1)} %param.28) | copy-start | bytes 1156
  7.2 21.3 %copy-start.41 = (s32[255]{0:T(256)S(1)}, s32[255]{0:T(256)}, u32[]{:S(2)}) copy-start(s32[255]{0:T(256)} %param.33) | copy-start | bytes 3064
  7.3 62.5 %all-gather.10.cloned.1.call-start = ((), (), s32[]{:S(2)}) async-start(), calls=%async_computation.8 | async-start | bytes 1474560 | tf_op jit(solution)/shard_map/all_gather | solution.py:286
  8.0 65.0 %all-gather.14.cloned.1.call-start = ((), (), s32[]{:S(2)}) async-start(), calls=%async_computation.10 | async-start | bytes 1474560 | tf_op jit(solution)/shard_map/all_gather | solution.py:286
  8.7 20.9 %copy-start.34 = (s32[1,2048]{1,0:T(1,128)S(1)}, s32[1,2048]{1,0:T(1,128)}, u32[]{:S(2)}) copy-start(s32[1,2048]{1,0:T(1,128)} %param.31) | copy-start | bytes 24580
  8.7 68.7 %all-gather.12.cloned.1.call-start = ((), (), s32[]{:S(2)}) async-start(), calls=%async_computation.9 | async-start | bytes 1474560 | tf_op jit(solution)/shard_map/all_gather | solution.py:286
  9.5 102.9 %all-gather.16.cloned.1.call-start = ((), (), s32[]{:S(2)}) async-start(), calls=%async_computation.11 | async-start | bytes 1474560 | tf_op jit(solution)/shard_map/all_gather | solution.py:286
  10.1 21.0 %copy-start.38 = (s32[1023]{0:T(1024)S(1)}, s32[1023]{0:T(1024)}, u32[]{:S(2)}) copy-start(s32[1023]{0:T(1024)} %param.32) | copy-start | bytes 12280
  10.1 106.7 %all-gather.18.cloned.1.call-start = ((), (), s32[]{:S(2)}) async-start(), calls=%async_computation.12 | async-start | bytes 3932160 | tf_op jit(solution)/shard_map/all_gather | solution.py:286
  10.7 136.1 %all-gather.20.cloned.1.call-start = ((), (), s32[]{:S(2)}) async-start(), calls=%async_computation.13 | async-start | bytes 3932160 | tf_op jit(solution)/shard_map/all_gather | solution.py:286
  11.2 165.6 %all-gather.22.cloned.1.call-start = ((), (), s32[]{:S(2)}) async-start(), calls=%async_computation.14 | async-start | bytes 3932160 | tf_op jit(solution)/shard_map/all_gather | solution.py:286
  11.3 57.2 %collective-permute-start = (bf16[256,768]{1,0:T(8,128)(2,1)S(1)}, bf16[256,768]{1,0:T(8,128)(2,1)S(1)}, u32[]{:S(2)}, u32[]{:S(2)}) collective-permute-start(bf16[256,768]{1,0:T(8,128)(2,1)S(1)} %bitcast.132), channel_id=1, source_target_pairs={{0,8},{4,12},{8,16},{12,20},{16,24},{20,28},{1,9},{5,13},{9,17},{1... | collective-permute-start | bytes 1179656 | tf_op jit(solution)/shard_map/ppermute | solution.py:25
  16.3 52.2 %collective-permute-start.1 = (bf16[256,768]{1,0:T(8,128)(2,1)S(1)}, bf16[256,768]{1,0:T(8,128)(2,1)S(1)}, u32[]{:S(2)}, u32[]{:S(2)}) collective-permute-start(bf16[256,768]{1,0:T(8,128)(2,1)S(1)} %bitcast.133), channel_id=1, source_target_pairs={{0,4},{4,8},{8,12},{12,16},{16,20},{20,24},{24,28},{1,5},{5,9},{9,... | collective-permute-start | bytes 1179656 | tf_op jit(solution)/shard_map/ppermute | solution.py:25
  19.7 48.9 %collective-permute-start.2 = (bf16[256,768]{1,0:T(8,128)(2,1)S(1)}, bf16[256,768]{1,0:T(8,128)(2,1)S(1)}, u32[]{:S(2)}, u32[]{:S(2)}) collective-permute-start(bf16[256,768]{1,0:T(8,128)(2,1)S(1)} %bitcast.134), channel_id=1, source_target_pairs={{4,0},{8,4},{12,8},{16,12},{20,16},{24,20},{28,24},{5,1},{9,5},{13... | collective-permute-start | bytes 1179656 | tf_op jit(solution)/shard_map/ppermute | solution.py:25
  21.0 47.6 %collective-permute-start.3 = (bf16[256,768]{1,0:T(8,128)(2,1)S(1)}, bf16[256,768]{1,0:T(8,128)(2,1)S(1)}, u32[]{:S(2)}, u32[]{:S(2)}) collective-permute-start(bf16[256,768]{1,0:T(8,128)(2,1)S(1)} %bitcast.135), channel_id=1, source_target_pairs={{8,0},{12,4},{16,8},{20,12},{24,16},{28,20},{9,1},{13,5},{17,9},{2... | collective-permute-start | bytes 1179656 | tf_op jit(solution)/shard_map/ppermute | solution.py:25
  22.4 240.8 %reduce-scatter.14.cloned.1.call-start = ((), (), s32[]{:S(2)}) async-start(), calls=%async_computation.18 | async-start | bytes 1474560 | tf_op jit(solution)/shard_map/reduce_scatter | solution.py:416
  29.0 201.8 %copy-start.25 = (f32[768]{0:T(1024)}, f32[768]{0:T(1024)S(1)}, u32[]{:S(2)}) copy-start(f32[768]{0:T(1024)S(1)} %reshape.274) | copy-start | bytes 9220
  29.0 201.8 %copy-start.30 = (f32[256]{0:T(256)}, f32[256]{0:T(256)S(1)}, u32[]{:S(2)}) copy-start(f32[256]{0:T(256)S(1)} %add_rsqrt_fusion.2) | copy-start | bytes 3076
  29.4 39.3 %copy-start.13 = (f32[16,768]{1,0:T(8,128)}, f32[16,768]{1,0:T(8,128)S(1)}, u32[]{:S(2)}) copy-start(f32[16,768]{1,0:T(8,128)S(1)} %convert_reduce_fusion) | copy-start | bytes 147460
  29.5 39.1 %copy-start.36 = (f32[16]{0:T(128)}, f32[16]{0:T(128)S(1)}, u32[]{:S(2)}) copy-start(f32[16]{0:T(128)S(1)} %add_rsqrt_fusion.3) | copy-start | bytes 196
  29.6 39.1 %copy-start.28 = (f32[768]{0:T(1024)}, f32[768]{0:T(1024)S(1)}, u32[]{:S(2)}) copy-start(f32[768]{0:T(1024)S(1)} %reshape.276) | copy-start | bytes 9220
  67.8 9.7 %copy-start.23 = (bf16[128,768]{1,0:T(8,128)(2,1)}, bf16[128,768]{1,0:T(8,128)(2,1)S(1)}, u32[]{:S(2)}) copy-start(bf16[128,768]{1,0:T(8,128)(2,1)S(1)} %all_gather.29) | copy-start | bytes 589828
  69.7 7.8 %copy-start.8 = (bf16[1280,768]{1,0:T(8,128)(2,1)}, bf16[1280,768]{1,0:T(8,128)(2,1)S(1)}, u32[]{:S(2)}) copy-start(bf16[1280,768]{1,0:T(8,128)(2,1)S(1)} %fusion.2) | copy-start | bytes 5898244
  121.0 55.9 %copy-start.9 = (bf16[1,256,768]{2,1,0:T(8,128)(2,1)S(1)}, bf16[1,256,768]{2,1,0:T(8,128)(2,1)}, u32[]{:S(2)}) copy-start(bf16[1,256,768]{2,1,0:T(8,128)(2,1)} %param.18) | copy-start | bytes 1179652
  190.3 73.0 %reduce-scatter.10.cloned.1.call-start = ((), (), s32[]{:S(2)}) async-start(), calls=%async_computation.16 | async-start | bytes 1474560 | tf_op jit(solution)/shard_map/reduce_scatter | solution.py:416
  191.6 28.5 %copy-start.24 = (bf16[128,768]{1,0:T(8,128)(2,1)S(1)}, bf16[128,768]{1,0:T(8,128)(2,1)}, u32[]{:S(2)}) copy-start(bf16[128,768]{1,0:T(8,128)(2,1)} %copy-done.23) | copy-start | bytes 589828
  225.3 54.4 %reduce-scatter.12.cloned.1.call-start = ((), (), s32[]{:S(2)}) async-start(), calls=%async_computation.17 | async-start | bytes 1474560 | tf_op jit(solution)/shard_map/reduce_scatter | solution.py:416
  230.7 77.8 %reduce-scatter.8.cloned.1.call-start = ((), (), s32[]{:S(2)}) async-start(), calls=%async_computation.15 | async-start | bytes 1474560 | tf_op jit(solution)/shard_map/reduce_scatter | solution.py:416
  232.5 116.4 %reduce-scatter.16.cloned.1.call-start = ((), (), s32[]{:S(2)}) async-start(), calls=%async_computation.19 | async-start | bytes 3932160 | tf_op jit(solution)/shard_map/reduce_scatter | solution.py:416
  236.5 152.8 %reduce-scatter.18.cloned.1.call-start = ((), (), s32[]{:S(2)}) async-start(), calls=%async_computation.20 | async-start | bytes 3932160 | tf_op jit(solution)/shard_map/reduce_scatter | solution.py:416
  240.5 189.1 %reduce-scatter.20.cloned.1.call-start = ((), (), s32[]{:S(2)}) async-start(), calls=%async_computation.21 | async-start | bytes 3932160 | tf_op jit(solution)/shard_map/reduce_scatter | solution.py:416
  244.7 350.0 %all-reduce.21.cloned.1.call-start = ((), (), s32[]{:S(2)}) async-start(), calls=%async_computation.22 | async-start | bytes 7077888 | tf_op jit(solution)/shard_map/psum | solution.py:420
  245.1 7.3 %copy-start.43 = (s32[143]{0:T(256)S(1)}, s32[143]{0:T(256)}, u32[]{:S(2)}) copy-start(s32[143]{0:T(256)} %copy-done.42) | copy-start | bytes 1720
  438.6 62.8 %collective-permute-start.4 = (bf16[256,768]{1,0:T(8,128)(2,1)}, bf16[256,768]{1,0:T(8,128)(2,1)}, u32[]{:S(2)}, u32[]{:S(2)}) collective-permute-start(bf16[256,768]{1,0:T(8,128)(2,1)} %get-tuple-element.45), channel_id=1, source_target_pairs={{4,0},{8,4},{12,8},{16,12},{20,16},{24,20},{28,24},{5,1},{9,5},{13... | collective-permute-start | bytes 1179656 | tf_op jit(solution)/shard_map/ppermute | solution.py:25
  439.9 61.5 %collective-permute-start.5 = (bf16[256,768]{1,0:T(8,128)(2,1)}, bf16[256,768]{1,0:T(8,128)(2,1)}, u32[]{:S(2)}, u32[]{:S(2)}) collective-permute-start(bf16[256,768]{1,0:T(8,128)(2,1)} %get-tuple-element.48), channel_id=1, source_target_pairs={{0,4},{4,8},{8,12},{12,16},{16,20},{20,24},{24,28},{1,5},{5,9},{9,... | collective-permute-start | bytes 1179656 | tf_op jit(solution)/shard_map/ppermute | solution.py:25
  445.2 56.1 %collective-permute-start.6 = (bf16[256,768]{1,0:T(8,128)(2,1)}, bf16[256,768]{1,0:T(8,128)(2,1)}, u32[]{:S(2)}, u32[]{:S(2)}) collective-permute-start(bf16[256,768]{1,0:T(8,128)(2,1)} %get-tuple-element.47), channel_id=1, source_target_pairs={{8,0},{12,4},{16,8},{20,12},{24,16},{28,20},{9,1},{13,5},{17,9},{2... | collective-permute-start | bytes 1179656 | tf_op jit(solution)/shard_map/ppermute | solution.py:25
  446.5 54.9 %collective-permute-start.7 = (bf16[256,768]{1,0:T(8,128)(2,1)}, bf16[256,768]{1,0:T(8,128)(2,1)}, u32[]{:S(2)}, u32[]{:S(2)}) collective-permute-start(bf16[256,768]{1,0:T(8,128)(2,1)} %get-tuple-element.46), channel_id=1, source_target_pairs={{0,8},{4,12},{8,16},{12,20},{16,24},{20,28},{1,9},{5,13},{9,17},{1... | collective-permute-start | bytes 1179656 | tf_op jit(solution)/shard_map/ppermute | solution.py:25
  451.9 48.2 %all-to-all-start = ((bf16[8,16,768]{2,1,0:T(8,128)(2,1)}), bf16[8,16,768]{2,1,0:T(8,128)(2,1)}, u32[]{:S(2)}, u32[]{:S(2)}) async-start(bf16[8,16,768]{2,1,0:T(8,128)(2,1)} %bitcast.6), calls=%async_computation | async-start | bytes 393216 | tf_op jit(solution)/shard_map/all_to_all | solution.py:388
  456.6 44.5 %copy-start.14 = (f32[16,768]{1,0:T(8,128)S(1)}, f32[16,768]{1,0:T(8,128)}, u32[]{:S(2)}) copy-start(f32[16,768]{1,0:T(8,128)} %copy-done.13) | copy-start | bytes 147460
  456.6 44.5 %copy-start.29 = (f32[768]{0:T(1024)S(1)}, f32[768]{0:T(1024)}, u32[]{:S(2)}) copy-start(f32[768]{0:T(1024)} %copy-done.28) | copy-start | bytes 9220
  456.6 44.5 %copy-start.37 = (f32[16]{0:T(128)S(1)}, f32[16]{0:T(128)}, u32[]{:S(2)}) copy-start(f32[16]{0:T(128)} %copy-done.36) | copy-start | bytes 196
  456.6 44.8 %copy-start.12 = (bf16[256,768]{1,0:T(8,128)(2,1)S(1)}, bf16[256,768]{1,0:T(8,128)(2,1)}, u32[]{:S(2)}) copy-start(bf16[256,768]{1,0:T(8,128)(2,1)} %get-tuple-element.23) | copy-start | bytes 1179652
  456.6 44.8 %copy-start.26 = (f32[768]{0:T(1024)S(1)}, f32[768]{0:T(1024)}, u32[]{:S(2)}) copy-start(f32[768]{0:T(1024)} %copy-done.25) | copy-start | bytes 9220
  456.6 44.8 %copy-start.31 = (f32[256]{0:T(256)S(1)}, f32[256]{0:T(256)}, u32[]{:S(2)}) copy-start(f32[256]{0:T(256)} %copy-done.30) | copy-start | bytes 3076
  (23 other events, 63.2 us)
Sparse Core Ops, SparseCore 0:
  9.6 20.2 all-gather.9
  31.4 17.3 all-gather.13
  50.4 17.4 all-gather.11
  69.3 17.3 all-gather.15
  88.2 28.5 all-gather.17
  118.2 28.4 all-gather.19
  148.3 28.4 all-gather.21
  190.4 25.6 reduce-scatter.13
  225.5 25.6 reduce-scatter.9
  254.1 25.6 reduce-scatter.11
  282.9 25.6 reduce-scatter.7
  310.9 37.8 reduce-scatter.15
  351.4 37.8 reduce-scatter.17
  391.7 37.8 reduce-scatter.19
  433.9 160.7 all-reduce.20

commit v2 on v1

--- a/solution.py
+++ b/solution.py
@@ -19,10 +19,86 @@
 VMEM_LIMIT = 60 << 20
 
 
+CTX = ("z", "y")
+SHARD = ("x", "c")
+
+
 def shifted(value, axis, by):
     length = lax.axis_size(axis)
     pairs = [(i, i + by) for i in range(length) if 0 <= i + by < length]
     return lax.ppermute(value, axis, pairs)
+
+
+def swapped(value, axis, bit=1):
+    return lax.ppermute(value, axis, [(i, i ^ bit) for i in range(lax.axis_size(axis))])
+
+
+def pick(value, index, dim=0):
+    return lax.dynamic_index_in_dim(value, index, dim, keepdims=False)
+
+
+def bit_of(axis, bit):
+    return (lax.axis_index(axis) // bit) % 2
+
+
+def halves(value):
+    return value.reshape(2, value.shape[0] // 2, *value.shape[1:])
+
+
+def in_order(own, other, upper):
+    return jnp.where(
+        upper == 1, jnp.concatenate([other, own], axis=0), jnp.concatenate([own, other], axis=0)
+    )
+
+
+def add_low(left, right):
+    return (left.astype(jnp.float32) + right.astype(jnp.float32)).astype(jnp.bfloat16)
+
+
+def bits(axis):
+    return [1 << k for k in range(lax.axis_size(axis).bit_length() - 1)]
+
+
+def scatter_over(value, axis, order):
+    for bit in order:
+        both, mine = halves(value), bit_of(axis, bit)
+        value = add_low(pick(both, mine), swapped(pick(both, 1 - mine), axis, bit))
+    return value
+
+
+def gather_over(value, axis, order):
+    for bit in order:
+        value = in_order(value, swapped(value, axis, bit), bit_of(axis, bit))
+    return value
+
+
+def over_lines(value):
+    order = bits("z")
+    value = scatter_over(value, "z", order)
+    value = gather_over(value, "z", order[::-1])
+    return gather_over(value, "y", [1])
+
+
+def core_sums(grads, rows):
+    core = lax.axis_index("c")
+    split = [a.astype(jnp.bfloat16).reshape(2, 2, r, a.shape[1]) for a, r in zip(grads, rows)]
+    got = [swapped(pick(a, 1 - core, 1), "c") for a in split]
+    return [add_low(pick(a, core, 1), b) for a, b in zip(split, got)]
+
+
+def scatter_planes(both):
+    x, y = lax.axis_index("x"), lax.axis_index("y")
+    cut = both.shape[3] // 2
+    first, second = both[..., :cut], both[..., cut:]
+    got_first = swapped(pick(first, 1 - x, 0), "x")
+    got_second = swapped(pick(second, 1 - y, 1), "y")
+    first = add_low(pick(first, x, 0), got_first)
+    second = add_low(pick(second, y, 1), got_second)
+    got_first = swapped(pick(first, 1 - y, 0), "y")
+    got_second = swapped(pick(second, 1 - x, 0), "x")
+    first = add_low(pick(first, y, 0), got_first)
+    second = add_low(pick(second, x, 0), got_second)
+    return jnp.concatenate([first, second], axis=1)
 
 
 def dot_nn(left, right):
@@ -271,21 +347,25 @@
     x_own = hidden[0]
     cot = cotangent[0]
     rows, width = x_own.shape
-    cycle_size = lax.axis_size("ctx")
-    cycle_index = lax.axis_index("ctx")
+    cycle_size = lax.axis_size(CTX)
+    cycle_index = lax.axis_index(CTX)
     first_row = cycle_index * rows
     far_len = rows * cycle_size // GB
     own_blocks = rows // GB
     reach = HALF // rows
     near_len = rows + 2 * HALF
 
-    left = [shifted(x_own, "ctx", d) for d in range(reach, 0, -1)]
-    right = [shifted(x_own, "ctx", -d) for d in range(1, reach + 1)]
+    left = [shifted(x_own, CTX, d) for d in range(reach, 0, -1)]
+    right = [shifted(x_own, CTX, -d) for d in range(1, reach + 1)]
     window = jnp.concatenate(left + [x_own] + right, axis=0)
 
-    gather = lambda a: lax.all_gather(a, "shard", axis=0, tiled=True)
-    w_query, w_key, w_value, w_out = map(gather, (query_proj, key_proj, value_proj, out_proj))
-    w_gate, w_up, w_down = map(gather, (gate_proj, up_proj, down_proj))
+    gather = lambda a: lax.all_gather(a, SHARD, axis=0, tiled=True)
+    whole = lambda a: a.reshape(-1, a.shape[-1])
+    first_set = gather(jnp.stack([query_proj, key_proj, value_proj, out_proj])[None])
+    w_query, w_key, w_value, w_out = [whole(first_set[:, i]) for i in range(4)]
+    second_set = gather(jnp.stack([gate_proj, up_proj])[None])
+    w_gate, w_up = [whole(second_set[:, i]) for i in range(2)]
+    w_down = gather(down_proj)
     small = jnp.concatenate(
         [first_gain, second_gain, global_gain, local_bias.reshape(-1), side_bias.reshape(-1)]
     )
@@ -339,7 +419,7 @@
     scale_side = rms_scale(block_sums)
     normed_side = block_sums * scale_side
     side_rows = (normed_side * gain_side).astype(jnp.bfloat16)
-    all_rows = lax.all_gather(side_rows, "ctx", axis=0, tiled=True)
+    all_rows = gather_over(gather_over(side_rows, "y", [1]), "z", bits("z"))
     key_rows = jnp.concatenate([normed_wide, all_rows], axis=0)
     queries = dot_nn(normed, w_query).astype(jnp.bfloat16)
     keys = dot_nn(key_rows, w_key).astype(jnp.bfloat16)
@@ -371,10 +451,13 @@
     dq, dk, dv, diag, dfar = attention_backward(
         queries, keys, values, attended_grad, attended, logs, q_label, k_label, base, far
     )
+    far_back = dot_nt(dk[near_len:], w_key) + dot_nt(dv[near_len:], w_value)
+    side_back = scatter_over(far_back.astype(jnp.bfloat16), "z", bits("z")[::-1])
+    side_back = scatter_over(side_back, "y", [1]).astype(jnp.float32)
     query_grad = dot_tn(normed, dq)
     key_grad = dot_tn(key_rows, dk)
     value_grad = dot_tn(key_rows, dv)
-    key_back = dot_nt(dk, w_key) + dot_nt(dv, w_value)
+    key_back = dot_nt(dk[:near_len], w_key) + dot_nt(dv[:near_len], w_value)
     own_start = reach * rows
     normed_back = dot_nt(dq, w_query) + key_back[own_start : own_start + rows]
     back_low = key_back.astype(jnp.bfloat16)
@@ -382,11 +465,8 @@
         for direction in (1, -1):
             at = (reach - direction * distance) * rows
             normed_back = normed_back + shifted(
-                back_low[at : at + rows], "ctx", -direction * distance
+                back_low[at : at + rows], CTX, -direction * distance
             ).astype(jnp.float32)
-    side_blocks = back_low[near_len:].reshape(cycle_size, own_blocks, width)
-    side_blocks = lax.all_to_all(side_blocks, "ctx", 0, 0, tiled=True)
-    side_back = jnp.sum(side_blocks.astype(jnp.float32), axis=0)
     global_part = jnp.sum(side_back * normed_side, axis=0)
     sums_grad = norm_back(side_back, normed_side, scale_side, gain_side)
     normed_back = (
@@ -413,32 +493,44 @@
         onehot_side.astype(jnp.float32), side_sum, (((0,), (1,)), ((), ())), precision=HIGHEST
     )
 
-    scatter = lambda a: lax.psum_scatter(
-        a.astype(jnp.bfloat16), "shard", scatter_dimension=0, tiled=True
-    )
-    big = [scatter(a) for a in (query_grad, key_grad, value_grad, out_grad, gate_grad, up_grad, down_grad)]
-    big = [lax.psum(a, "ctx").astype(jnp.float32) for a in big]
+    cut, deep = query_proj.shape[0], down_proj.shape[0]
+    plane = lambda a: lax.psum_scatter(a, ("x", "y"), scatter_dimension=0, tiled=True)
+    (down_sum,) = core_sums([down_grad], [deep])
+    down_sum = over_lines(plane(whole(down_sum)))
+    pair = jnp.stack(core_sums([gate_grad, up_grad], [cut] * 2), axis=1)
+    pair = over_lines(plane(whole(pair))).reshape(2, cut, -1)
+    four = jnp.stack(core_sums([query_grad, key_grad, value_grad, out_grad], [cut] * 4), axis=1)
+    four = over_lines(scatter_planes(four.reshape(2, 2, 2 * cut, -1))).reshape(4, cut, -1)
+    big = [four[0], four[1], four[2], four[3], pair[0], pair[1], down_sum]
+    big = [a.astype(jnp.float32) for a in big]
     tiny = jnp.concatenate(
         [a.reshape(-1) for a in (first_part, second_part, global_part, local_part, side_part)]
-    )
-    tiny = lax.psum(tiny.reshape(-1, LANES), ("ctx", "shard")).reshape(-1)
-    shard = lax.axis_index("shard")
+    ).reshape(-1, LANES)
+    for axis in ("c", "x", "y", "z"):
+        for bit in bits(axis):
+            tiny = tiny + swapped(tiny, axis, bit)
+    tiny = tiny.reshape(-1)
+    shard = lax.axis_index(SHARD)
     done, at = [], 0
     for a in (first_part, second_part, global_part, local_part, side_part):
-        whole = tiny[at : at + a.size].reshape(a.shape)
+        whole_sum = tiny[at : at + a.size].reshape(a.shape)
         at += a.size
-        part = a.shape[0] // lax.axis_size("shard")
-        done.append(lax.dynamic_slice_in_dim(whole, shard * part, part, 0))
+        part = a.shape[0] // lax.axis_size(SHARD)
+        done.append(lax.dynamic_slice_in_dim(whole_sum, shard * part, part, 0))
     return (outputs[None], hidden_grad[None], *big, *done)
 
 
 def solution(mesh):
-    tokens = P("shard", "ctx", None)
-    weight = P("shard", None)
-    gain = P("shard")
+    ctx, shard = mesh.shape["ctx"], mesh.shape["shard"]
+    fine = jax.sharding.Mesh(
+        mesh.devices.reshape(ctx // 2, 2, shard // 2, 2), CTX + SHARD
+    )
+    tokens = P(SHARD, CTX, None)
+    weight = P(SHARD, None)
+    gain = P(SHARD)
     return jax.shard_map(
         on_device,
-        mesh=mesh,
+        mesh=fine,
         in_specs=(tokens, tokens) + (weight,) * 7 + (gain,) * 3 + (weight,) * 3 + (P(), P()),
         out_specs=(tokens, tokens) + (weight,) * 7 + (gain,) * 3 + (weight,) * 2,
         check_vma=False,

time: 611 us -> 419 us (0.69); the launches traced: 610 us -> 411 us
  waiting for transfers between devices: 310 us -> 133 us
  blocking collectives: 79.6 us -> 5.37 us
  starting transfers between devices: 29.8 us -> 61.4 us
  local copies, waits for them, and re-layouts: 22.6 us -> 46.2 us
  matrix products: 78.9 us -> 60.8 us
  other arithmetic: 15.6 us -> 30.1 us
    reduce_scatter x7 -> x2, waiting for transfers between devices: 166 us -> 0.01 us  [on_device(): lax.psum_scatter(a, ('x', 'y'), scatter_dimension=0, tiled=True)]
    ppermute x0 -> x37, waiting for transfers between devices: none -> 110 us  [swapped(): lax.ppermute(value, axis, [(i, i ^ bit) for i in range(lax.axis_size(axis...]
    psum x1 -> x0, waiting for transfers between devices: 45.7 us -> none  [on_device(): big = [lax.psum(a, 'ctx').astype(jnp.float32) for a in big]]
    psum x1 -> x0, blocking collectives: 40.3 us -> none  [on_device(): tiny = lax.psum(tiny.reshape(-1, LANES), ('ctx', 'shard')).reshape(-1)]
    all_to_all x1 -> x0, waiting for transfers between devices: 39.8 us -> none  [on_device(): side_blocks = lax.all_to_all(side_blocks, 'ctx', 0, 0, tiled=True)]
    ppermute x0 -> x37, starting transfers between devices: none -> 37.3 us  [swapped(): lax.ppermute(value, axis, [(i, i ^ bit) for i in range(lax.axis_size(axis...]
    all_gather x2 -> x1, blocking collectives: 39.3 us -> 5.37 us  [on_device(): gather = lambda a: lax.all_gather(a, SHARD, axis=0, tiled=True)]
    all_gather x7 -> x3, waiting for transfers between devices: 53.8 us -> 22.9 us  [on_device(): gather = lambda a: lax.all_gather(a, SHARD, axis=0, tiled=True)]
  transfers between devices with their start and end apart: 24 -> 50, of which waited for: 10 -> 25; matrix products, arithmetic and copies ran while one was open for 15% -> 18% of each run, Pallas kernels for 10% -> 8%
where the time goes in v2:
time: 419 us; the launch traced here: 411 us
  waiting for transfers between devices  133 us (32%)
  starting transfers between devices  61.4 us (15%)
  matrix products  60.8 us (15%)
  Pallas kernels  59.2 us (14%)
  local copies, waits for them, and re-layouts  46.2 us (11%)
  other arithmetic  30.1 us (7%)
  between operations  15.5 us (4%)
  blocking collectives  5.37 us (1%)
    ppermute x37, waiting for transfers between devices, swapped(): lax.ppermute(value, axis, [(i, i ^ bit) for i in range(lax.axis_size(axis...  110 us
    ppermute x37, starting transfers between devices, swapped(): lax.ppermute(value, axis, [(i, i ^ bit) for i in range(lax.axis_size(axis...  37.3 us
    pallas_call x1, Pallas kernels, attention_forward(): pl.pallas_call(forward_kernel, grid=(PAIRS,), in_specs=[s['q'], s['k'], s...  30.9 us
    pallas_call x1, Pallas kernels, attention_backward(): pl.pallas_call(backward_kernel, grid=(PAIRS,), in_specs=[s['q'], s['k'],...  28.3 us
    dot_general x9, matrix products, dot_nt(): lax.dot_general(left, right, (((1,), (1,)), ((), ())), preferred_element_...  26.3 us
    ppermute x8, starting transfers between devices, shifted(): return lax.ppermute(value, axis, pairs)  23.6 us
    all_gather x3, waiting for transfers between devices, on_device(): gather = lambda a: lax.all_gather(a, SHARD, axis=0, tiled=True)  22.9 us
    dot_general x7, matrix products, dot_nn(): lax.dot_general(left, right, (((1,), (0,)), ((), ())), preferred_element_...  16.1 us
  transfers between devices with their start and end apart: 50, of which 25 were waited for; matrix products, arithmetic and copies ran while one was open for 18% of the time, Pallas kernels for 8%

profile of v2, /device:TPU:0, one launch (start us, length us, event | category | flops | bytes accessed | tf_op | source)
XLA Modules:
  0.0 411.4 jit_solution(3234437449001029432)
XLA Ops:
  7.2 2.5 pad_maximum_fusion.4
  11.3 5.0 %collective-permute-start = (bf16[256,768]{1,0:T(8,128)(2,1)S(1)}, bf16[256,768]{1,0:T(8,128)(2,1)S(1)}, u32[]{:S(2)}, u32[]{:S(2)}) collective-permute-start(bf16[256,768]{1,0:T(8,128)(2,1)S(1)} %bitcast.299), channel_id=1, source_target_pairs={{0,8},{4,12},{8,16},{12,20},{16,24},{20,28},{1,9},{5,13},{9,17},{1... | collective-permute-start | bytes 1179656 | tf_op jit(solution)/shard_map/ppermute | solution.py:29
  16.3 3.4 collective-permute-start.1
  22.6 5.4 %all-gather.3 = bf16[4,1,768]{2,1,0:T(2,128)(2,1)S(1)} all-gather(bf16[1,1,768]{2,1,0:T(2,128)(2,1)S(1)} %reshape.389), channel_id=2, replica_groups=mesh['z'=4,'y'=2,'x'=2,'c'=2] {'x','c'}, dimensions={0}, use_global_device_ids=true | all-gather | bytes 7680 | tf_op jit(solution)/shard_map/all_gather | solution.py:362
  29.5 2.6 collective-permute-start.4
  34.5 2.2 collective-permute-done.4
  36.7 5.7 %collective-permute-start.5 = (bf16[32,768]{1,0:T(8,128)(2,1)S(1)}, bf16[32,768]{1,0:T(8,128)(2,1)S(1)}, u32[]{:S(2)}, u32[]{:S(2)}) collective-permute-start(bf16[32,768]{1,0:T(8,128)(2,1)S(1)} %maximum_select_fusion.11), channel_id=1, source_target_pairs={{0,8},{8,0},{16,24},{24,16},{1,9},{9,1},{17,25},{25,17},{2,10},{10... | collective-permute-start | bytes 147464 | tf_op jit(solution)/shard_map/ppermute | solution.py:33
  42.5 2.1 collective-permute-done.5
  44.6 3.1 collective-permute-start.6
  52.2 3.4 fusion.140
  57.3 3.2 convolution_convert_fusion.3.v_ref
  60.5 3.2 convolution_convert_fusion.4.k_ref
  63.7 30.9 %attention_forward.1 = (bf16[256,768]{1,0:T(8,128)(2,1)}, f32[6,256,128]{2,1,0:T(8,128)}) custom-call(bf16[256,768]{1,0:T(8,128)(2,1)} %convolution_convert_fusion.10.q_ref, bf16[1408,768]{1,0:T(8,128)(2,1)} %convolution_convert_fusion.4.k_ref, bf16[1408,768]{1,0:T(8,128)(2,1)} %convolution_convert_fusion.3.v_ref, bf16[256,128]{1,0:T(8,128)(2,1)} %fusion.76.q_label_ref, ...), custom_call_target="tpu_custom_call" | custom-call | tf_op jit(solution)/shard_map/attention_forward/pallas_call | solution.py:288
  98.9 3.5 fusion.139
  102.4 2.3 fusion.149
  104.8 2.3 fusion.150
  107.1 22.0 %all-gather.8.cloned.1.call-done = bf16[2048,768]{1,0:T(8,128)(2,1)} async-done(((bf16[512,768]{1,0:T(8,128)(2,1)}), bf16[2048,768]{1,0:T(8,128)(2,1)}) %all-gather.8.cloned.1.call-update) | async-done | bytes 3145744 | tf_op jit(solution)/shard_map/all_gather | solution.py:362
  129.0 6.6 %multiply_convert_fusion = (bf16[256,2048]{1,0:T(8,128)(2,1)S(1)}, bf16[256,2048]{1,0:T(8,128)(2,1)S(1)}, bf16[256,2048]{1,0:T(8,128)(2,1)}) fusion(f32[256,2048]{1,0:T(8,128)} %fusion.149, f32[256,2048]{1,0:T(8,128)} %fusion.150, bf16[2048,768]{1,0:T(8,128)(2,1)} %all-gather.8.cloned.1.call-done, bf16[1,256,768]{2,1,0:T(8,128)(2,1)} %param.18), kind=kOutput, calls=%fused_computation.29 | convolution fusion | flops 818937856 | bytes 10878976 | tf_op jit(solution)/shard_map/dot_general | solution.py:111
  141.8 28.3 %attention_backward.1 = (bf16[256,768]{1,0:T(8,128)(2,1)}, bf16[1408,768]{1,0:T(8,128)(2,1)}, bf16[1408,768]{1,0:T(8,128)(2,1)}, f32[6,2,8,1408]{3,2,1,0:T(8,128)}, f32[6,2,16,128]{3,2,1,0:T(8,128)}) custom-call(bf16[256,768]{1,0:T(8,128)(2,1)} %convolution_convert_fusion.10.q_ref, bf16[1408,768]{1,0:T(8,128)(2,1)} %convolution_convert_fusion.4.k_ref, ...), custom_call_target="tpu_custom_call" | custom-call | tf_op jit(solution)/shard_map/attention_backward/pallas_call | solution.py:311
  170.2 4.2 %fusion.143 = (f32[12,1,1408]{2,1,0:T(1,128)}, f32[12,1,1408]{2,1,0:T(1,128)S(1)}, f32[12,1,1408]{2,1,0:T(1,128)S(1)}, f32[12,1,1408]{2,1,0:T(1,128)S(1)}, f32[1...) fusion(f32[12,8,1408]{2,1,0:T(8,128)} %bitcast.343), kind=kLoop, calls=%fused_computation.307 | loop fusion | bytes 1081344 | tf_op jit(solution)/shard_map/slice | solution.py:481
  183.7 3.7 fusion.14
  188.8 2.6 convolution_convert_fusion.2
  198.2 2.4 fusion.64
  202.0 6.8 %fusion.148 = (bf16[1280,768]{1,0:T(8,128)(2,1)S(1)}, f32[1280,768]{1,0:T(8,128)}) fusion(f32[1280,768]{1,0:T(8,128)} %fusion.14, bf16[768,768]{1,0:T(8,128)(2,1)} %bitcast.308, bf16[1408,768]{1,0:T(8,128)(2,1)} %get-tuple-element.25), kind=kOutput, calls=%fused_computation.312 | convolution fusion | flops 1511915520 | bytes 12976128 | tf_op jit(solution)/shard_map/dot_general | solution.py:111
  210.0 4.3 %collective-permute-start.10 = (bf16[256,768]{1,0:T(8,128)(2,1)}, bf16[256,768]{1,0:T(8,128)(2,1)}, u32[]{:S(2)}, u32[]{:S(2)}) collective-permute-start(bf16[256,768]{1,0:T(8,128)(2,1)} %get-tuple-element.48), channel_id=1, source_target_pairs={{0,8},{4,12},{8,16},{12,20},{16,24},{20,28},{1,9},{5,13},{9,17},{1... | collective-permute-start | bytes 1179656 | tf_op jit(solution)/shard_map/ppermute | solution.py:29
  215.5 5.5 %collective-permute-start.8 = (bf16[256,768]{1,0:T(8,128)(2,1)}, bf16[256,768]{1,0:T(8,128)(2,1)}, u32[]{:S(2)}, u32[]{:S(2)}) collective-permute-start(bf16[256,768]{1,0:T(8,128)(2,1)} %get-tuple-element.50), channel_id=1, source_target_pairs={{0,4},{4,8},{8,12},{12,16},{16,20},{20,24},{24,28},{1,5},{5,9},{9,... | collective-permute-start | bytes 1179656 | tf_op jit(solution)/shard_map/ppermute | solution.py:29
  227.7 3.1 convolution_convert_fusion.7
  230.8 3.1 convolution_convert_fusion.6
  236.1 2.3 collective-permute-start.11
  241.4 10.3 %collective-permute-done.11 = bf16[64,768]{1,0:T(8,128)(2,1)} collective-permute-done((bf16[64,768]{1,0:T(8,128)(2,1)}, bf16[64,768]{1,0:T(8,128)(2,1)}, u32[]{:S(2)}, u32[]{:S(2)}) %collective-permute-start.11) | collective-permute-done | bytes 98336 | tf_op jit(solution)/shard_map/ppermute | solution.py:33
  253.9 2.9 collective-permute-done.12
  256.8 2.3 collective-permute-start.13
  262.6 3.4 fusion.37
  268.1 3.1 collective-permute-done.41
  271.2 2.1 collective-permute-start.42
  282.2 14.3 %collective-permute-done.18 = bf16[2,384,384]{2,1,0:T(8,128)(2,1)S(1)} collective-permute-done((bf16[2,384,384]{2,1,0:T(8,128)(2,1)S(1)}, bf16[2,384,384]{2,1,0:T(8,128)(2,1)S(1)}, u32[]{:S(2)}, u32[]{:S(2)}) %collective-permute-start.18) | collective-permute-done | bytes 589856 | tf_op jit(solution)/shard_map/ppermute | solution.py:33
  302.3 4.3 %collective-permute-done.19 = bf16[384,384]{1,0:T(8,128)(2,1)} collective-permute-done((bf16[384,384]{1,0:T(8,128)(2,1)}, bf16[384,384]{1,0:T(8,128)(2,1)}, u32[]{:S(2)}, u32[]{:S(2)}) %collective-permute-start.19) | collective-permute-done | bytes 294944 | tf_op jit(solution)/shard_map/ppermute | solution.py:33
  313.2 4.5 %collective-permute-done.22 = bf16[192,768]{1,0:T(8,128)(2,1)S(1)} collective-permute-done((bf16[192,768]{1,0:T(8,128)(2,1)S(1)}, bf16[192,768]{1,0:T(8,128)(2,1)S(1)}, u32[]{:S(2)}, u32[]{:S(2)}) %collective-permute-start.22) | collective-permute-done | bytes 294944 | tf_op jit(solution)/shard_map/ppermute | solution.py:33
  326.5 7.7 %collective-permute-done.29 = bf16[96,2048]{1,0:T(8,128)(2,1)S(1)} collective-permute-done((bf16[96,2048]{1,0:T(8,128)(2,1)S(1)}, bf16[96,2048]{1,0:T(8,128)(2,1)S(1)}, u32[]{:S(2)}, u32[]{:S(2)}) %collective-permute-start.29) | collective-permute-done | bytes 393248 | tf_op jit(solution)/shard_map/ppermute | solution.py:33
  336.3 2.5 collective-permute-start.25
  339.9 5.9 %collective-permute-done.30 = bf16[48,2048]{1,0:T(8,128)(2,1)S(1)} collective-permute-done((bf16[48,2048]{1,0:T(8,128)(2,1)S(1)}, bf16[48,2048]{1,0:T(8,128)(2,1)S(1)}, u32[]{:S(2)}, u32[]{:S(2)}) %collective-permute-start.30) | collective-permute-done | bytes 196640 | tf_op jit(solution)/shard_map/ppermute | solution.py:33
  345.9 9.7 %collective-permute-done.35 = bf16[128,768]{1,0:T(8,128)(2,1)S(1)} collective-permute-done((bf16[128,768]{1,0:T(8,128)(2,1)S(1)}, bf16[128,768]{1,0:T(8,128)(2,1)S(1)}, u32[]{:S(2)}, u32[]{:S(2)}) %collective-permute-start.35) | collective-permute-done | bytes 196640 | tf_op jit(solution)/shard_map/ppermute | solution.py:33
  357.0 2.2 collective-permute-done.31
  359.7 3.4 collective-permute-done.36
  364.8 5.1 %collective-permute-done.37 = bf16[64,768]{1,0:T(8,128)(2,1)S(1)} collective-permute-done((bf16[64,768]{1,0:T(8,128)(2,1)S(1)}, bf16[64,768]{1,0:T(8,128)(2,1)S(1)}, u32[]{:S(2)}, u32[]{:S(2)}) %collective-permute-start.37) | collective-permute-done | bytes 98336 | tf_op jit(solution)/shard_map/ppermute | solution.py:33
  373.2 2.5 collective-permute-done.38
  376.1 4.1 collective-permute-done.26
  382.0 18.4 %collective-permute-done.39 = bf16[256,768]{1,0:T(8,128)(2,1)S(1)} collective-permute-done((bf16[256,768]{1,0:T(8,128)(2,1)S(1)}, bf16[256,768]{1,0:T(8,128)(2,1)S(1)}, u32[]{:S(2)}, u32[]{:S(2)}) %collective-permute-start.39) | collective-permute-done | bytes 393248 | tf_op jit(solution)/shard_map/ppermute | solution.py:33
  (419 shorter events, 111.3 us)
Async XLA Ops:
  7.2 45.0 %all-gather.10.cloned.1.call-start = ((), (), s32[]{:S(2)}) async-start(), calls=%async_computation.5 | async-start | bytes 5898240 | tf_op jit(solution)/shard_map/all_gather | solution.py:362
  9.8 89.2 %all-gather.12.cloned.1.call-start = ((), (), s32[]{:S(2)}) async-start(), calls=%async_computation.6 | async-start | bytes 7864320 | tf_op jit(solution)/shard_map/all_gather | solution.py:362
  11.2 117.8 %all-gather.8.cloned.1.call-start = ((), (), s32[]{:S(2)}) async-start(), calls=%async_computation.2 | async-start | bytes 3932160 | tf_op jit(solution)/shard_map/all_gather | solution.py:362
  11.3 39.7 %collective-permute-start = (bf16[256,768]{1,0:T(8,128)(2,1)S(1)}, bf16[256,768]{1,0:T(8,128)(2,1)S(1)}, u32[]{:S(2)}, u32[]{:S(2)}) collective-permute-start(bf16[256,768]{1,0:T(8,128)(2,1)S(1)} %bitcast.299), channel_id=1, source_target_pairs={{0,8},{4,12},{8,16},{12,20},{16,24},{20,28},{1,9},{5,13},{9,17},{1... | collective-permute-start | bytes 1179656 | tf_op jit(solution)/shard_map/ppermute | solution.py:29
  16.3 34.7 %collective-permute-start.1 = (bf16[256,768]{1,0:T(8,128)(2,1)S(1)}, bf16[256,768]{1,0:T(8,128)(2,1)S(1)}, u32[]{:S(2)}, u32[]{:S(2)}) collective-permute-start(bf16[256,768]{1,0:T(8,128)(2,1)S(1)} %bitcast.300), channel_id=1, source_target_pairs={{0,4},{4,8},{8,12},{12,16},{16,20},{20,24},{24,28},{1,5},{5,9},{9,... | collective-permute-start | bytes 1179656 | tf_op jit(solution)/shard_map/ppermute | solution.py:29
  19.7 31.4 %collective-permute-start.2 = (bf16[256,768]{1,0:T(8,128)(2,1)S(1)}, bf16[256,768]{1,0:T(8,128)(2,1)S(1)}, u32[]{:S(2)}, u32[]{:S(2)}) collective-permute-start(bf16[256,768]{1,0:T(8,128)(2,1)S(1)} %bitcast.301), channel_id=1, source_target_pairs={{4,0},{8,4},{12,8},{16,12},{20,16},{24,20},{28,24},{5,1},{9,5},{13... | collective-permute-start | bytes 1179656 | tf_op jit(solution)/shard_map/ppermute | solution.py:29
  21.0 30.1 %collective-permute-start.3 = (bf16[256,768]{1,0:T(8,128)(2,1)S(1)}, bf16[256,768]{1,0:T(8,128)(2,1)S(1)}, u32[]{:S(2)}, u32[]{:S(2)}) collective-permute-start(bf16[256,768]{1,0:T(8,128)(2,1)S(1)} %bitcast.302), channel_id=1, source_target_pairs={{8,0},{12,4},{16,8},{20,12},{24,16},{28,20},{9,1},{13,5},{17,9},{2... | collective-permute-start | bytes 1179656 | tf_op jit(solution)/shard_map/ppermute | solution.py:29
  29.5 7.3 %collective-permute-start.4 = (bf16[16,768]{1,0:T(8,128)(2,1)S(1)}, bf16[16,768]{1,0:T(8,128)(2,1)S(1)}, u32[]{:S(2)}, u32[]{:S(2)}) collective-permute-start(bf16[16,768]{1,0:T(8,128)(2,1)S(1)} %multiply_convert_fusion.5), channel_id=1, source_target_pairs={{0,4},{4,0},{1,5},{5,1},{2,6},{6,2},{3,7},{7,3},{8,12},{12,8},{9,1... | collective-permute-start | bytes 73736 | tf_op jit(solution)/shard_map/ppermute | solution.py:33
  32.1 286.0 %reduce-scatter.3.cloned.1.call-start = ((), (), s32[]{:S(2)}) async-start(), calls=%async_computation.3 | async-start | bytes 3932160 | tf_op jit(solution)/shard_map/reduce_scatter | solution.py:497
  36.7 7.8 %collective-permute-start.5 = (bf16[32,768]{1,0:T(8,128)(2,1)S(1)}, bf16[32,768]{1,0:T(8,128)(2,1)S(1)}, u32[]{:S(2)}, u32[]{:S(2)}) collective-permute-start(bf16[32,768]{1,0:T(8,128)(2,1)S(1)} %maximum_select_fusion.11), channel_id=1, source_target_pairs={{0,8},{8,0},{16,24},{24,16},{1,9},{9,1},{17,25},{25,17},{2,10},{10... | collective-permute-start | bytes 147464 | tf_op jit(solution)/shard_map/ppermute | solution.py:33
  44.6 6.3 %collective-permute-start.6 = (bf16[64,768]{1,0:T(8,128)(2,1)S(1)}, bf16[64,768]{1,0:T(8,128)(2,1)S(1)}, u32[]{:S(2)}, u32[]{:S(2)}) collective-permute-start(bf16[64,768]{1,0:T(8,128)(2,1)S(1)} %maximum_select_fusion.10), channel_id=1, source_target_pairs={{0,16},{8,24},{16,0},{24,8},{1,17},{9,25},{17,1},{25,9},{2,18},{10... | collective-permute-start | bytes 294920 | tf_op jit(solution)/shard_map/ppermute | solution.py:33
  210.0 51.9 %collective-permute-start.10 = (bf16[256,768]{1,0:T(8,128)(2,1)}, bf16[256,768]{1,0:T(8,128)(2,1)}, u32[]{:S(2)}, u32[]{:S(2)}) collective-permute-start(bf16[256,768]{1,0:T(8,128)(2,1)} %get-tuple-element.48), channel_id=1, source_target_pairs={{0,8},{4,12},{8,16},{12,20},{16,24},{20,28},{1,9},{5,13},{9,17},{1... | collective-permute-start | bytes 1179656 | tf_op jit(solution)/shard_map/ppermute | solution.py:29
  214.2 48.2 %collective-permute-start.7 = (bf16[256,768]{1,0:T(8,128)(2,1)}, bf16[256,768]{1,0:T(8,128)(2,1)}, u32[]{:S(2)}, u32[]{:S(2)}) collective-permute-start(bf16[256,768]{1,0:T(8,128)(2,1)} %get-tuple-element.47), channel_id=1, source_target_pairs={{4,0},{8,4},{12,8},{16,12},{20,16},{24,20},{28,24},{5,1},{9,5},{13... | collective-permute-start | bytes 1179656 | tf_op jit(solution)/shard_map/ppermute | solution.py:29
  215.5 47.0 %collective-permute-start.8 = (bf16[256,768]{1,0:T(8,128)(2,1)}, bf16[256,768]{1,0:T(8,128)(2,1)}, u32[]{:S(2)}, u32[]{:S(2)}) collective-permute-start(bf16[256,768]{1,0:T(8,128)(2,1)} %get-tuple-element.50), channel_id=1, source_target_pairs={{0,4},{4,8},{8,12},{12,16},{16,20},{20,24},{24,28},{1,5},{5,9},{9,... | collective-permute-start | bytes 1179656 | tf_op jit(solution)/shard_map/ppermute | solution.py:29
  221.2 12.7 %collective-permute-start.27 = (bf16[2,192,2048]{2,1,0:T(8,128)(2,1)S(1)}, bf16[2,192,2048]{2,1,0:T(8,128)(2,1)S(1)}, u32[]{:S(2)}, u32[]{:S(2)}) collective-permute-start(bf16[2,192,2048]{2,1,0:T(8,128)(2,1)S(1)} %dynamic-slice_bitcast_fusion.2), channel_id=1, source_target_pairs={{0,1},{1,0},{2,3},{3,2},{4,5},{5,4},{6,7},{7,6},{8,9},{9,8},{10,11... | collective-permute-start | bytes 4718600 | tf_op jit(solution)/shard_map/ppermute | solution.py:33
  221.4 14.7 %collective-permute-start.28 = (bf16[2,192,2048]{2,1,0:T(8,128)(2,1)S(1)}, bf16[2,192,2048]{2,1,0:T(8,128)(2,1)S(1)}, u32[]{:S(2)}, u32[]{:S(2)}) collective-permute-start(bf16[2,192,2048]{2,1,0:T(8,128)(2,1)S(1)} %dynamic-slice_bitcast_fusion.1), channel_id=1, source_target_pairs={{0,1},{1,0},{2,3},{3,2},{4,5},{5,4},{6,7},{7,6},{8,9},{9,8},{10,11... | collective-permute-start | bytes 4718600 | tf_op jit(solution)/shard_map/ppermute | solution.py:33
  233.9 28.6 %collective-permute-start.9 = (bf16[256,768]{1,0:T(8,128)(2,1)}, bf16[256,768]{1,0:T(8,128)(2,1)}, u32[]{:S(2)}, u32[]{:S(2)}) collective-permute-start(bf16[256,768]{1,0:T(8,128)(2,1)} %get-tuple-element.49), channel_id=1, source_target_pairs={{8,0},{12,4},{16,8},{20,12},{24,16},{28,20},{9,1},{13,5},{17,9},{2... | collective-permute-start | bytes 1179656 | tf_op jit(solution)/shard_map/ppermute | solution.py:29
  236.1 15.5 %collective-permute-start.11 = (bf16[64,768]{1,0:T(8,128)(2,1)}, bf16[64,768]{1,0:T(8,128)(2,1)}, u32[]{:S(2)}, u32[]{:S(2)}) collective-permute-start(bf16[64,768]{1,0:T(8,128)(2,1)} %dynamic-slice_bitcast_fusion.17), channel_id=1, source_target_pairs={{0,16},{8,24},{16,0},{24,8},{1,17},{9,25},{17,1},{25,9},{2,18},{10... | collective-permute-start | bytes 294920 | tf_op jit(solution)/shard_map/ppermute | solution.py:33
  241.0 97.8 %reduce-scatter.5.cloned.1.call-start = ((), (), s32[]{:S(2)}) async-start(), calls=%async_computation.4 | async-start | bytes 1966080 | tf_op jit(solution)/shard_map/reduce_scatter | solution.py:497
  252.6 4.2 %collective-permute-start.12 = (bf16[32,768]{1,0:T(8,128)(2,1)S(1)}, bf16[32,768]{1,0:T(8,128)(2,1)S(1)}, u32[]{:S(2)}, u32[]{:S(2)}) collective-permute-start(bf16[32,768]{1,0:T(8,128)(2,1)S(1)} %dynamic-slice_bitcast_fusion.18), channel_id=1, source_target_pairs={{0,8},{8,0},{16,24},{24,16},{1,9},{9,1},{17,25},{25,17},{2,10},{10... | collective-permute-start | bytes 147464 | tf_op jit(solution)/shard_map/ppermute | solution.py:33
  256.8 4.7 %collective-permute-start.13 = (bf16[16,768]{1,0:T(8,128)(2,1)S(1)}, bf16[16,768]{1,0:T(8,128)(2,1)S(1)}, u32[]{:S(2)}, u32[]{:S(2)}) collective-permute-start(bf16[16,768]{1,0:T(8,128)(2,1)S(1)} %dynamic-slice_bitcast_fusion.19), channel_id=1, source_target_pairs={{0,4},{4,0},{1,5},{5,1},{2,6},{6,2},{3,7},{7,3},{8,12},{12,8},{9,1... | collective-permute-start | bytes 73736 | tf_op jit(solution)/shard_map/ppermute | solution.py:33
  261.5 39.1 %collective-permute-start.34 = (bf16[2,512,768]{2,1,0:T(8,128)(2,1)}, bf16[2,512,768]{2,1,0:T(8,128)(2,1)S(1)}, u32[]{:S(2)}, u32[]{:S(2)}) collective-permute-start(bf16[2,512,768]{2,1,0:T(8,128)(2,1)} %dynamic-slice_bitcast_fusion), channel_id=1, source_target_pairs={{0,1},{1,0},{2,3},{3,2},{4,5},{5,4},{6,7},{7,6},{8,9},{9,8},{10,11... | collective-permute-start | bytes 4718600 | tf_op jit(solution)/shard_map/ppermute | solution.py:33
  261.9 9.3 %collective-permute-start.14 = (bf16[2,192,768]{2,1,0:T(8,128)(2,1)S(1)}, bf16[2,192,768]{2,1,0:T(8,128)(2,1)S(1)}, u32[]{:S(2)}, u32[]{:S(2)}) collective-permute-start(bf16[2,192,768]{2,1,0:T(8,128)(2,1)S(1)} %dynamic-slice_bitcast_fusion.8), channel_id=1, source_target_pairs={{0,1},{1,0},{2,3},{3,2},{4,5},{5,4},{6,7},{7,6},{8,9},{9,8},{10,11... | collective-permute-start | bytes 1769480 | tf_op jit(solution)/shard_map/ppermute | solution.py:33
  262.4 11.0 %collective-permute-start.15 = (bf16[2,192,768]{2,1,0:T(8,128)(2,1)S(1)}, bf16[2,192,768]{2,1,0:T(8,128)(2,1)S(1)}, u32[]{:S(2)}, u32[]{:S(2)}) collective-permute-start(bf16[2,192,768]{2,1,0:T(8,128)(2,1)S(1)} %dynamic-slice_bitcast_fusion.7), channel_id=1, source_target_pairs={{0,1},{1,0},{2,3},{3,2},{4,5},{5,4},{6,7},{7,6},{8,9},{9,8},{10,11... | collective-permute-start | bytes 1769480 | tf_op jit(solution)/shard_map/ppermute | solution.py:33
  266.7 7.0 %collective-permute-start.16 = (bf16[2,192,768]{2,1,0:T(8,128)(2,1)S(1)}, bf16[2,192,768]{2,1,0:T(8,128)(2,1)S(1)}, u32[]{:S(2)}, u32[]{:S(2)}) collective-permute-start(bf16[2,192,768]{2,1,0:T(8,128)(2,1)S(1)} %dynamic-slice_bitcast_fusion.6), channel_id=1, source_target_pairs={{0,1},{1,0},{2,3},{3,2},{4,5},{5,4},{6,7},{7,6},{8,9},{9,8},{10,11... | collective-permute-start | bytes 1769480 | tf_op jit(solution)/shard_map/ppermute | solution.py:33
  267.5 3.7 collective-permute-start.41
  271.2 7.3 %collective-permute-start.42 = (f32[24,128]{1,0:T(8,128)S(1)}, f32[24,128]{1,0:T(8,128)S(1)}, u32[]{:S(2)}, u32[]{:S(2)}) collective-permute-start(f32[24,128]{1,0:T(8,128)S(1)} %fusion.186), channel_id=1, source_target_pairs={{0,4},{4,0},{1,5},{5,1},{2,6},{6,2},{3,7},{7,3},{8,12},{12,8},{9,1... | collective-permute-start | bytes 36872 | tf_op jit(solution)/shard_map/ppermute | solution.py:33
  274.7 21.9 %collective-permute-start.18 = (bf16[2,384,384]{2,1,0:T(8,128)(2,1)S(1)}, bf16[2,384,384]{2,1,0:T(8,128)(2,1)S(1)}, u32[]{:S(2)}, u32[]{:S(2)}) collective-permute-start(bf16[2,384,384]{2,1,0:T(8,128)(2,1)S(1)} %dynamic-slice_bitcast_fusion.4), channel_id=1, source_target_pairs={{0,2},{2,0},{1,3},{3,1},{4,6},{6,4},{5,7},{7,5},{8,10},{10,8},{9,1... | collective-permute-start | bytes 1769480 | tf_op jit(solution)/shard_map/ppermute | solution.py:33
  278.5 3.7 collective-permute-start.43
  279.1 19.9 %collective-permute-start.20 = (bf16[2,384,384]{2,1,0:T(8,128)(2,1)S(1)}, bf16[2,384,384]{2,1,0:T(8,128)(2,1)S(1)}, u32[]{:S(2)}, u32[]{:S(2)}) collective-permute-start(bf16[2,384,384]{2,1,0:T(8,128)(2,1)S(1)} %dynamic-slice_bitcast_fusion.3), channel_id=1, source_target_pairs={{0,4},{4,0},{1,5},{5,1},{2,6},{6,2},{3,7},{7,3},{8,12},{12,8},{9,1... | collective-permute-start | bytes 1769480 | tf_op jit(solution)/shard_map/ppermute | solution.py:33
  282.2 30.3 %collective-permute-start.44 = (f32[24,128]{1,0:T(8,128)S(1)}, f32[24,128]{1,0:T(8,128)}, u32[]{:S(2)}, u32[]{:S(2)}) collective-permute-start(f32[24,128]{1,0:T(8,128)S(1)} %add.498), channel_id=1, source_target_pairs={{0,16},{8,24},{16,0},{24,8},{1,17},{9,25},{17,1},{25,9},{2,18},{10... | collective-permute-start | bytes 36872 | tf_op jit(solution)/shard_map/ppermute | solution.py:33
  297.5 9.1 %collective-permute-start.19 = (bf16[384,384]{1,0:T(8,128)(2,1)}, bf16[384,384]{1,0:T(8,128)(2,1)}, u32[]{:S(2)}, u32[]{:S(2)}) collective-permute-start(bf16[384,384]{1,0:T(8,128)(2,1)} %dynamic-slice_bitcast_fusion.12), channel_id=1, source_target_pairs={{0,4},{4,0},{1,5},{5,1},{2,6},{6,2},{3,7},{7,3},{8,12},{12,8},{9,1... | collective-permute-start | bytes 884744 | tf_op jit(solution)/shard_map/ppermute | solution.py:33
  300.1 8.8 %collective-permute-start.21 = (bf16[384,384]{1,0:T(8,128)(2,1)}, bf16[384,384]{1,0:T(8,128)(2,1)}, u32[]{:S(2)}, u32[]{:S(2)}) collective-permute-start(bf16[384,384]{1,0:T(8,128)(2,1)} %dynamic-slice_bitcast_fusion.11), channel_id=1, source_target_pairs={{0,2},{2,0},{1,3},{3,1},{4,6},{6,4},{5,7},{7,5},{8,10},{10,8},{9,1... | collective-permute-start | bytes 884744 | tf_op jit(solution)/shard_map/ppermute | solution.py:33
  310.0 7.7 %collective-permute-start.22 = (bf16[192,768]{1,0:T(8,128)(2,1)S(1)}, bf16[192,768]{1,0:T(8,128)(2,1)S(1)}, u32[]{:S(2)}, u32[]{:S(2)}) collective-permute-start(bf16[192,768]{1,0:T(8,128)(2,1)S(1)} %dynamic-slice_bitcast_fusion.10), channel_id=1, source_target_pairs={{0,8},{8,0},{16,24},{24,16},{1,9},{9,1},{17,25},{25,17},{2,10},{10... | collective-permute-start | bytes 884744 | tf_op jit(solution)/shard_map/ppermute | solution.py:33
  317.9 7.0 %collective-permute-start.23 = (bf16[96,768]{1,0:T(8,128)(2,1)S(1)}, bf16[96,768]{1,0:T(8,128)(2,1)S(1)}, u32[]{:S(2)}, u32[]{:S(2)}) collective-permute-start(bf16[96,768]{1,0:T(8,128)(2,1)S(1)} %dynamic-slice_bitcast_fusion.15), channel_id=1, source_target_pairs={{0,16},{8,24},{16,0},{24,8},{1,17},{9,25},{17,1},{25,9},{2,18},{10... | collective-permute-start | bytes 442376 | tf_op jit(solution)/shard_map/ppermute | solution.py:33
  319.2 15.0 %collective-permute-start.29 = (bf16[96,2048]{1,0:T(8,128)(2,1)S(1)}, bf16[96,2048]{1,0:T(8,128)(2,1)S(1)}, u32[]{:S(2)}, u32[]{:S(2)}) collective-permute-start(bf16[96,2048]{1,0:T(8,128)(2,1)S(1)} %dynamic-slice_bitcast_fusion.9), channel_id=1, source_target_pairs={{0,8},{8,0},{16,24},{24,16},{1,9},{9,1},{17,25},{25,17},{2,10},{10... | collective-permute-start | bytes 1179656 | tf_op jit(solution)/shard_map/ppermute | solution.py:33
  324.9 11.3 %collective-permute-start.24 = (bf16[96,768]{1,0:T(8,128)(2,1)S(1)}, bf16[96,768]{1,0:T(8,128)(2,1)S(1)}, u32[]{:S(2)}, u32[]{:S(2)}) collective-permute-start(bf16[96,768]{1,0:T(8,128)(2,1)S(1)} %fusion.63), channel_id=1, source_target_pairs={{0,16},{8,24},{16,0},{24,8},{1,17},{9,25},{17,1},{25,9},{2,18},{10... | collective-permute-start | bytes 442376 | tf_op jit(solution)/shard_map/ppermute | solution.py:33
  335.3 10.5 %collective-permute-start.30 = (bf16[48,2048]{1,0:T(8,128)(2,1)S(1)}, bf16[48,2048]{1,0:T(8,128)(2,1)S(1)}, u32[]{:S(2)}, u32[]{:S(2)}) collective-permute-start(bf16[48,2048]{1,0:T(8,128)(2,1)S(1)} %dynamic-slice_bitcast_fusion.14), channel_id=1, source_target_pairs={{0,16},{8,24},{16,0},{24,8},{1,17},{9,25},{17,1},{25,9},{2,18},{10... | collective-permute-start | bytes 589832 | tf_op jit(solution)/shard_map/ppermute | solution.py:33
  336.3 27.4 %collective-permute-start.25 = (bf16[192,768]{1,0:T(8,128)(2,1)S(1)}, bf16[192,768]{1,0:T(8,128)(2,1)S(1)}, u32[]{:S(2)}, u32[]{:S(2)}) collective-permute-start(bf16[192,768]{1,0:T(8,128)(2,1)S(1)} %maximum_select_fusion.7), channel_id=1, source_target_pairs={{0,8},{8,0},{16,24},{24,16},{1,9},{9,1},{17,25},{25,17},{2,10},{10... | collective-permute-start | bytes 884744 | tf_op jit(solution)/shard_map/ppermute | solution.py:33
  339.8 15.8 %collective-permute-start.35 = (bf16[128,768]{1,0:T(8,128)(2,1)S(1)}, bf16[128,768]{1,0:T(8,128)(2,1)S(1)}, u32[]{:S(2)}, u32[]{:S(2)}) collective-permute-start(bf16[128,768]{1,0:T(8,128)(2,1)S(1)} %dynamic-slice_bitcast_fusion.13), channel_id=1, source_target_pairs={{0,8},{8,0},{16,24},{24,16},{1,9},{9,1},{17,25},{25,17},{2,10},{10... | collective-permute-start | bytes 589832 | tf_op jit(solution)/shard_map/ppermute | solution.py:33
  345.9 13.4 %collective-permute-start.31 = (bf16[48,2048]{1,0:T(8,128)(2,1)S(1)}, bf16[48,2048]{1,0:T(8,128)(2,1)S(1)}, u32[]{:S(2)}, u32[]{:S(2)}) collective-permute-start(bf16[48,2048]{1,0:T(8,128)(2,1)S(1)} %fusion.55), channel_id=1, source_target_pairs={{0,16},{8,24},{16,0},{24,8},{1,17},{9,25},{17,1},{25,9},{2,18},{10... | collective-permute-start | bytes 589832 | tf_op jit(solution)/shard_map/ppermute | solution.py:33
  356.6 6.4 %collective-permute-start.36 = (bf16[64,768]{1,0:T(8,128)(2,1)S(1)}, bf16[64,768]{1,0:T(8,128)(2,1)S(1)}, u32[]{:S(2)}, u32[]{:S(2)}) collective-permute-start(bf16[64,768]{1,0:T(8,128)(2,1)S(1)} %dynamic-slice_bitcast_fusion.16), channel_id=1, source_target_pairs={{0,16},{8,24},{16,0},{24,8},{1,17},{9,25},{17,1},{25,9},{2,18},{10... | collective-permute-start | bytes 294920 | tf_op jit(solution)/shard_map/ppermute | solution.py:33
  359.4 13.0 %collective-permute-start.32 = (bf16[96,2048]{1,0:T(8,128)(2,1)S(1)}, bf16[96,2048]{1,0:T(8,128)(2,1)S(1)}, u32[]{:S(2)}, u32[]{:S(2)}) collective-permute-start(bf16[96,2048]{1,0:T(8,128)(2,1)S(1)} %maximum_select_fusion.5), channel_id=1, source_target_pairs={{0,8},{8,0},{16,24},{24,16},{1,9},{9,1},{17,25},{25,17},{2,10},{10... | collective-permute-start | bytes 1179656 | tf_op jit(solution)/shard_map/ppermute | solution.py:33
  363.1 6.8 %collective-permute-start.37 = (bf16[64,768]{1,0:T(8,128)(2,1)S(1)}, bf16[64,768]{1,0:T(8,128)(2,1)S(1)}, u32[]{:S(2)}, u32[]{:S(2)}) collective-permute-start(bf16[64,768]{1,0:T(8,128)(2,1)S(1)} %fusion.68), channel_id=1, source_target_pairs={{0,16},{8,24},{16,0},{24,8},{1,17},{9,25},{17,1},{25,9},{2,18},{10... | collective-permute-start | bytes 294920 | tf_op jit(solution)/shard_map/ppermute | solution.py:33
  363.9 16.3 %collective-permute-start.26 = (bf16[384,768]{1,0:T(8,128)(2,1)S(1)}, bf16[384,768]{1,0:T(8,128)(2,1)S(1)}, u32[]{:S(2)}, u32[]{:S(2)}) collective-permute-start(bf16[384,768]{1,0:T(8,128)(2,1)S(1)} %maximum_select_fusion.4), channel_id=1, source_target_pairs={{0,4},{4,0},{1,5},{5,1},{2,6},{6,2},{3,7},{7,3},{8,12},{12,8},{9,1... | collective-permute-start | bytes 1769480 | tf_op jit(solution)/shard_map/ppermute | solution.py:33
  369.9 5.7 %collective-permute-start.38 = (bf16[128,768]{1,0:T(8,128)(2,1)S(1)}, bf16[128,768]{1,0:T(8,128)(2,1)S(1)}, u32[]{:S(2)}, u32[]{:S(2)}) collective-permute-start(bf16[128,768]{1,0:T(8,128)(2,1)S(1)} %maximum_select_fusion.9), channel_id=1, source_target_pairs={{0,8},{8,0},{16,24},{24,16},{1,9},{9,1},{17,25},{25,17},{2,10},{10... | collective-permute-start | bytes 589832 | tf_op jit(solution)/shard_map/ppermute | solution.py:33
  372.5 29.4 %collective-permute-start.33 = (bf16[192,2048]{1,0:T(8,128)(2,1)S(1)}, bf16[192,2048]{1,0:T(8,128)(2,1)S(1)}, u32[]{:S(2)}, u32[]{:S(2)}) collective-permute-start(bf16[192,2048]{1,0:T(8,128)(2,1)S(1)} %maximum_select_fusion.2), channel_id=1, source_target_pairs={{0,4},{4,0},{1,5},{5,1},{2,6},{6,2},{3,7},{7,3},{8,12},{12,8},{9,1... | collective-permute-start | bytes 2359304 | tf_op jit(solution)/shard_map/ppermute | solution.py:33
  375.8 24.7 %collective-permute-start.39 = (bf16[256,768]{1,0:T(8,128)(2,1)S(1)}, bf16[256,768]{1,0:T(8,128)(2,1)S(1)}, u32[]{:S(2)}, u32[]{:S(2)}) collective-permute-start(bf16[256,768]{1,0:T(8,128)(2,1)S(1)} %maximum_select_fusion.6), channel_id=1, source_target_pairs={{0,4},{4,0},{1,5},{5,1},{2,6},{6,2},{3,7},{7,3},{8,12},{12,8},{9,1... | collective-permute-start | bytes 1179656 | tf_op jit(solution)/shard_map/ppermute | solution.py:33
  (80 other events, 781.0 us)
Sparse Core Ops, SparseCore 0:
  10.1 40.2 all-gather.9
  52.5 46.3 all-gather.11
  100.5 28.4 all-gather.7
  241.2 50.4 reduce-scatter.2
  302.4 29.3 reduce-scatter.4
